TPU v7x, 256 devices: a whole 4x4x8 slice. The times are simulated.
256 devices in a mesh: tile: 64 (over z, x, core), height: 4 (over y).
Axes of the slice: x: 4, y: 4, z: 8, core: 2. Of those that a mesh axis runs over, the one named last changes fastest.
Arguments:
- material: int32 [32, 2048, 128], P('height', 'tile'), may hold values from 0 to 2
- clamped: int32 [32, 2048, 128], P('height', 'tile'), may hold values from 0 to 1, as said below
- stiffness_table: float32 [3], replicated, may hold values from 0.5 to 4
- eigenstrain: float32 [3, 3], replicated, may hold values from -6 to 6
Outputs:
- displacement: float32 [3, 32, 2048, 128], P(None, 'height', 'tile')
Inputs may be any that keep to these rules, and one draw needn't show every extreme that they name: `clamped`: only voxels of the lowest 2 layers can be 1; in those layers 0 and 1 are equally likely.
All inputs are finite; a program needn't handle non-finite values.
Results may differ from a plain program's by a relative error of at most 0.00016.
Values sent between devices are 32-bit elements; how exact they have to be, the bound alone decides.
A program may use at most 128 MiB of HBM per device.

v0:
```python
import jax
import jax.numpy as jnp
from jax import lax
from jax.sharding import PartitionSpec as P

NLABEL = 3
LEVELS = 3
PRE = 2
COARSE_SWEEPS = 6


GAMMA = 1.0
PENALTY = 50.0
OMEGA = 0.6


def with_halo(block, sides, width):
    for axis, dim in sides:
        count = lax.axis_size(axis)
        forward = [(i, i + 1) for i in range(count - 1)]
        backward = [(target, source) for source, target in forward]
        low = lax.ppermute(
            lax.slice_in_dim(block, block.shape[dim] - width, None, axis=dim), axis, forward
        )
        high = lax.ppermute(lax.slice_in_dim(block, 0, width, axis=dim), axis, backward)
        block = jnp.concatenate([low, block, high], axis=dim)
    return block


def passed_along(x, axis, by):
    size = lax.axis_size(axis)
    pairs = [(i, i + by) for i in range(size) if 0 <= i + by < size]
    return lax.ppermute(x, axis, pairs)


def lookup(labels, table):
    result = jnp.zeros(labels.shape, table.dtype)
    for label_id in range(NLABEL):
        result = result + (labels == label_id).astype(table.dtype) * table[label_id]
    return result


def block_sum(field):
    dims_now = field.shape
    shaped = field.reshape(
        dims_now[0], dims_now[1] // 2, 2, dims_now[2] // 2, 2, dims_now[3] // 2, 2
    )
    return shaped.sum(axis=(2, 4, 6))


def prolong(field):
    return jnp.repeat(jnp.repeat(jnp.repeat(field, 2, axis=1), 2, axis=2), 2, axis=3)


def direction_factor(direction, dtype):
    return jnp.where(jnp.arange(3) == direction, 1.0 + GAMMA, 1.0).astype(dtype).reshape(3, 1, 1, 1)


def coefficients(stiffness, spring, pairs):
    k_lower, k_upper = ([], [])
    diagonal = jnp.broadcast_to(spring, (3,) + spring.shape[1:])
    for direction in range(3):
        lower_nb, upper_nb = pairs[direction]
        low_face = 0.5 * (stiffness + lower_nb)
        high_face = 0.5 * (stiffness + upper_nb)
        diagonal = diagonal + direction_factor(direction, stiffness.dtype) * (low_face + high_face)
        k_lower.append(low_face)
        k_upper.append(high_face)
    return (k_lower, k_upper, diagonal)


def apply_operator(motion, spring, k_lower, k_upper, pairs):
    result = spring * motion
    for direction in range(3):
        lower_nb, upper_nb = pairs[direction]
        term = k_lower[direction] * (motion - lower_nb) + k_upper[direction] * (motion - upper_nb)
        result = result + direction_factor(direction, motion.dtype) * term
    return result


def smooth_from_zero(source, spring, terms, sweeps, pairs_fn):
    k_lower, k_upper, diagonal = terms
    motion = OMEGA * source / diagonal
    for turn_idx in range(sweeps - 1):
        motion = (
            motion
            + OMEGA
            * (source - apply_operator(motion, spring, k_lower, k_upper, pairs_fn(motion)))
            / diagonal
        )
    return motion


def layer_slabs(field, width):
    extended = with_halo(field, (("height", 1),), width)
    total = extended.shape[1]
    return (
        lax.slice_in_dim(extended, 0, width, axis=1),
        lax.slice_in_dim(extended, total - width, total, axis=1),
    )


def row_slabs(field, width):
    edge = field.shape[2]
    slabs = []
    for offset in (1, -1):
        if offset > 0:
            sent = lax.slice_in_dim(field, edge - width, edge, axis=2)
        else:
            sent = lax.slice_in_dim(field, 0, width, axis=2)
        slabs.append(passed_along(sent, "tile", offset))
    return (slabs[0], slabs[1])


def column_slabs(field, width):
    empty = jnp.zeros(field.shape[:3] + (width,), field.dtype)
    return (empty, empty)


def face_pair(field, direction, width):
    if direction == 0:
        return layer_slabs(field, width)
    if direction == 1:
        return row_slabs(field, width)
    return column_slabs(field, width)


def neighbour_arrays(field, axis_dim, low_slab, high_slab):
    length = field.shape[axis_dim]
    lower_nb = jnp.concatenate(
        [low_slab, lax.slice_in_dim(field, 0, length - 1, axis=axis_dim)], axis=axis_dim
    )
    upper_nb = jnp.concatenate(
        [lax.slice_in_dim(field, 1, length, axis=axis_dim), high_slab], axis=axis_dim
    )
    return (lower_nb, upper_nb)


def local_pairs(field):
    pairs = []
    for direction in range(3):
        low_slab, high_slab = face_pair(field, direction, 1)
        pairs.append(neighbour_arrays(field, direction + 1, low_slab, high_slab))
    return pairs


def stiffness_pairs(stiffness):
    pairs = []
    for direction in range(3):
        low_slab, high_slab = face_pair(stiffness, direction, 1)
        pairs.append(neighbour_arrays(stiffness, direction + 1, low_slab, high_slab))
    return pairs


def local(material, clamped, stiffness_table, eigenstrain):
    labels = material[None]
    stiffness = lookup(labels, stiffness_table)
    spring = PENALTY * clamped[None].astype(jnp.float32)
    pieces = []
    for component in range(3):
        stress = stiffness * lookup(labels, eigenstrain[:, component])
        low_slab, high_slab = face_pair(stress, component, 1)
        lower_nb, upper_nb = neighbour_arrays(stress, component + 1, low_slab, high_slab)
        pieces.append(0.5 * (lower_nb - upper_nb))
    source = jnp.concatenate(pieces, 0)
    saved = []
    for grid_level in range(LEVELS):
        terms = coefficients(stiffness, spring, stiffness_pairs(stiffness))
        motion = smooth_from_zero(source, spring, terms, PRE, local_pairs)
        remain = source - apply_operator(motion, spring, terms[0], terms[1], local_pairs(motion))
        saved.append((motion, source, spring, terms))
        source = block_sum(remain)
        stiffness = 0.5 * block_sum(stiffness)
        spring = block_sum(spring)
    terms = coefficients(stiffness, spring, stiffness_pairs(stiffness))
    motion = smooth_from_zero(source, spring, terms, COARSE_SWEEPS, local_pairs)
    for grid_level in reversed(range(LEVELS)):
        level_motion, level_source, level_spring, terms = saved[grid_level]
        k_lower, k_upper, diagonal = terms
        motion = level_motion + prolong(motion)
        motion = (
            motion
            + OMEGA
            * (
                level_source
                - apply_operator(motion, level_spring, k_lower, k_upper, local_pairs(motion))
            )
            / diagonal
        )
    return motion


def solution(mesh):
    in_specs = (P("height", "tile", None), P("height", "tile", None), P(), P())
    out_specs = P(None, "height", "tile", None)
    return jax.shard_map(local, mesh=mesh, in_specs=in_specs, out_specs=out_specs, check_vma=False)
```

profile of v0, /device:TPU:103, one launch (start us, length us, event | category | flops | bytes accessed | tf_op | source)
XLA Modules:
  0.0 418.1 jit_solution(3718154904222270836)
XLA Ops:
  1.4 2.9 select_add_fusion
  8.8 9.8 %reshape.836 = f32[4,2,16,2,64,2]{5,4,3,2,1,0:T(8,128)} reshape(f32[8,32,128]{2,1,0:T(8,128)S(1)} %copy.176) | data formatting | bytes 262144 | tf_op jit(solution)/shard_map/reshape | solution.py:45
  18.6 4.0 reduce_sum.97
  23.9 4.0 collective-permute-start.16
  27.9 2.7 collective-permute-start.19
  30.7 6.1 %collective-permute-start.18 = (f32[1,4,1,64]{3,1,2,0:T(4,128)S(1)}, f32[1,4,1,64]{3,1,2,0:T(4,128)S(1)}, u32[]{:S(2)}, u32[]{:S(2)}) collective-permute-start(f32[1,4,1,64]{3,1,2,0:T(4,128)S(1)} %bitcast.178), channel_id=1, source_target_pairs={{0,4},{4,8},{8,12},{12,16},{16,20},{20,24},{24,28},{28,32},{32,36}... | collective-permute-start | bytes 3080 | tf_op jit(solution)/shard_map/ppermute | solution.py:33
  40.0 9.8 %reshape.835 = f32[4,2,16,2,64,2]{5,4,3,2,1,0:T(8,128)} reshape(f32[8,32,128]{2,1,0:T(8,128)S(1)} %get-tuple-element.64) | data formatting | bytes 262144 | tf_op jit(solution)/shard_map/reshape | solution.py:45
  49.8 4.0 reduce_sum.96
  62.5 4.0 collective-permute-start.28
  71.1 6.3 %collective-permute-start.30 = (f32[1,2,1,32]{3,2,1,0:T(1,128)S(1)}, f32[1,2,1,32]{3,2,1,0:T(1,128)S(1)}, u32[]{:S(2)}, u32[]{:S(2)}) collective-permute-start(f32[1,2,1,32]{3,2,1,0:T(1,128)S(1)} %get-tuple-element.170), channel_id=1, source_target_pairs={{0,4},{4,8},{8,12},{12,16},{16,20},{20,24},{24,28},{28,32},{32,36}... | collective-permute-start | bytes 776 | tf_op jit(solution)/shard_map/ppermute | solution.py:33
  79.4 4.0 collective-permute-start.4
  84.2 3.2 collective-permute-start.40
  89.4 7.0 %collective-permute-start.42 = (f32[1,1,1,16]{3,2,1,0:T(1,128)S(1)}, f32[1,1,1,16]{3,2,1,0:T(1,128)S(1)}, u32[]{:S(2)}, u32[]{:S(2)}) collective-permute-start(f32[1,1,1,16]{3,2,1,0:T(1,128)S(1)} %get-tuple-element.215), channel_id=1, source_target_pairs={{0,4},{4,8},{8,12},{12,16},{16,20},{20,24},{24,28},{28,32},{32,36}... | collective-permute-start | bytes 200 | tf_op jit(solution)/shard_map/ppermute | solution.py:33
  101.4 7.6 %fusion.226 = (f32[8,32,128]{2,0,1:T(8,128)S(1)}, f32[8,32,128]{2,0,1:T(8,128)S(1)}, f32[8,32,128]{2,0,1:T(8,128)S(1)}, f32[1,8,32,128]{3,1,2,0:T(8,128)S(1)}, f...) fusion(f32[1,32,128]{2,0,1:T(1,128)S(1)} %bitcast.166, f32[7,32,128]{2,0,1:T(8,128)S(1)} %get-tuple-element.78, ...), kind=kLoop, calls=%fused_computation.330 | loop fusion | flops 983040 | bytes 1146928 | tf_op jit(solution)/shard_map/add | solution.py:66
  109.2 4.4 %collective-permute-start.2 = (f32[1,8,1,128]{3,1,2,0:T(8,128)S(1)}, f32[1,8,1,128]{3,1,2,0:T(8,128)S(1)}, u32[]{:S(2)}, u32[]{:S(2)}) collective-permute-start(f32[1,8,1,128]{3,1,2,0:T(8,128)S(1)} %get-tuple-element.72), channel_id=1, source_target_pairs={{0,4},{4,8},{8,12},{12,16},{16,20},{20,24},{24,28},{28,32},{32,36}... | collective-permute-start | bytes 12296 | tf_op jit(solution)/shard_map/ppermute | solution.py:33
  115.6 3.2 collective-permute-start
  127.1 8.7 %collective-permute-start.10 = (f32[3,8,1,128]{3,1,2,0:T(8,128)S(1)}, f32[3,8,1,128]{3,1,2,0:T(8,128)S(1)}, u32[]{:S(2)}, u32[]{:S(2)}) collective-permute-start(f32[3,8,1,128]{3,1,2,0:T(8,128)S(1)} %get-tuple-element.55), channel_id=1, source_target_pairs={{0,4},{4,8},{8,12},{12,16},{16,20},{20,24},{24,28},{28,32},{32,36}... | collective-permute-start | bytes 36872 | tf_op jit(solution)/shard_map/ppermute | solution.py:33
  137.8 6.3 %collective-permute-done.11 = f32[3,8,1,128]{3,1,2,0:T(8,128)S(1)} collective-permute-done((f32[3,8,1,128]{3,1,2,0:T(8,128)S(1)}, f32[3,8,1,128]{3,1,2,0:T(8,128)S(1)}, u32[]{:S(2)}, u32[]{:S(2)}) %collective-permute-start.11) | collective-permute-done | bytes 12320 | tf_op jit(solution)/shard_map/ppermute | solution.py:33
  145.2 4.3 %collective-permute-start.12 = (f32[3,1,32,128]{3,1,2,0:T(1,128)S(1)}, f32[3,1,32,128]{3,1,2,0:T(1,128)S(1)}, u32[]{:S(2)}, u32[]{:S(2)}) collective-permute-start(f32[3,1,32,128]{3,1,2,0:T(1,128)S(1)} %get-tuple-element.49), channel_id=1, source_target_pairs={{0,1},{1,2},{2,3},{4,5},{5,6},{6,7},{8,9},{9,10},{10,11},{12,13},{... | collective-permute-start | bytes 147464 | tf_op jit(solution)/shard_map/ppermute | solution.py:22
  155.4 6.0 %collective-permute-done.15 = f32[3,8,1,128]{3,1,2,0:T(8,128)S(1)} collective-permute-done((f32[3,8,1,128]{3,1,2,0:T(8,128)S(1)}, f32[3,8,1,128]{3,1,2,0:T(8,128)S(1)}, u32[]{:S(2)}, u32[]{:S(2)}) %collective-permute-start.15) | collective-permute-done | bytes 12320 | tf_op jit(solution)/shard_map/ppermute | solution.py:33
  162.0 26.5 %reshape.834 = f32[3,4,2,16,2,64,2]{6,5,4,3,2,1,0:T(8,128)} reshape(f32[3,8,32,128]{3,2,1,0:T(8,128)S(1)} %copy.175) | data formatting | bytes 786432 | tf_op jit(solution)/shard_map/reshape | solution.py:45
  188.6 9.4 %reduce_sum.95 = f32[3,4,16,64]{3,2,1,0:T(8,128)S(1)} reduce(f32[3,4,2,16,2,64,2]{6,5,4,3,2,1,0:T(8,128)} %reshape.834, f32[]{:T(128)} %constant.13.clone.1), dimensions={2,4,6}, to_apply=%region_0.1 | reduce | flops 86016 | bytes 442372 | tf_op jit(solution)/shard_map/reduce_sum | solution.py:48
  198.3 4.3 %collective-permute-start.20 = (f32[3,1,16,64]{3,2,1,0:T(8,128)S(1)}, f32[3,1,16,64]{3,2,1,0:T(8,128)S(1)}, u32[]{:S(2)}, u32[]{:S(2)}) collective-permute-start(f32[3,1,16,64]{3,2,1,0:T(8,128)S(1)} %get-tuple-element.114), channel_id=1, source_target_pairs={{0,1},{1,2},{2,3},{4,5},{5,6},{6,7},{8,9},{9,10},{10,11},{12,13},{... | collective-permute-start | bytes 36872 | tf_op jit(solution)/shard_map/ppermute | solution.py:22
  208.2 6.1 %collective-permute-done.23 = f32[3,4,1,64]{3,2,1,0:T(1,128)S(1)} collective-permute-done((f32[3,4,1,64]{3,2,1,0:T(1,128)S(1)}, f32[3,4,1,64]{3,2,1,0:T(1,128)S(1)}, u32[]{:S(2)}, u32[]{:S(2)}) %collective-permute-start.23) | collective-permute-done | bytes 3104 | tf_op jit(solution)/shard_map/ppermute | solution.py:33
  214.7 4.3 %collective-permute-start.24 = (f32[3,1,16,64]{3,2,1,0:T(8,128)S(1)}, f32[3,1,16,64]{3,2,1,0:T(8,128)S(1)}, u32[]{:S(2)}, u32[]{:S(2)}) collective-permute-start(f32[3,1,16,64]{3,2,1,0:T(8,128)S(1)} %get-tuple-element.104), channel_id=1, source_target_pairs={{0,1},{1,2},{2,3},{4,5},{5,6},{6,7},{8,9},{9,10},{10,11},{12,13},{... | collective-permute-start | bytes 36872 | tf_op jit(solution)/shard_map/ppermute | solution.py:22
  224.7 6.1 %collective-permute-done.27 = f32[3,4,1,64]{3,2,1,0:T(1,128)S(1)} collective-permute-done((f32[3,4,1,64]{3,2,1,0:T(1,128)S(1)}, f32[3,4,1,64]{3,2,1,0:T(1,128)S(1)}, u32[]{:S(2)}, u32[]{:S(2)}) %collective-permute-start.27) | collective-permute-done | bytes 3104 | tf_op jit(solution)/shard_map/ppermute | solution.py:33
  231.7 4.1 reshape.837
  237.6 4.3 %collective-permute-start.32 = (f32[3,1,8,32]{3,2,1,0:T(8,128)S(1)}, f32[3,1,8,32]{3,2,1,0:T(8,128)S(1)}, u32[]{:S(2)}, u32[]{:S(2)}) collective-permute-start(f32[3,1,8,32]{3,2,1,0:T(8,128)S(1)} %get-tuple-element.157), channel_id=1, source_target_pairs={{0,1},{1,2},{2,3},{4,5},{5,6},{6,7},{8,9},{9,10},{10,11},{12,13},{... | collective-permute-start | bytes 9224 | tf_op jit(solution)/shard_map/ppermute | solution.py:22
  247.6 6.0 %collective-permute-done.35 = f32[3,2,1,32]{3,2,1,0:T(1,128)S(1)} collective-permute-done((f32[3,2,1,32]{3,2,1,0:T(1,128)S(1)}, f32[3,2,1,32]{3,2,1,0:T(1,128)S(1)}, u32[]{:S(2)}, u32[]{:S(2)}) %collective-permute-start.35) | collective-permute-done | bytes 800 | tf_op jit(solution)/shard_map/ppermute | solution.py:33
  254.7 4.3 %collective-permute-start.36 = (f32[3,1,8,32]{3,2,1,0:T(8,128)S(1)}, f32[3,1,8,32]{3,2,1,0:T(8,128)S(1)}, u32[]{:S(2)}, u32[]{:S(2)}) collective-permute-start(f32[3,1,8,32]{3,2,1,0:T(8,128)S(1)} %get-tuple-element.149), channel_id=1, source_target_pairs={{0,1},{1,2},{2,3},{4,5},{5,6},{6,7},{8,9},{9,10},{10,11},{12,13},{... | collective-permute-start | bytes 9224 | tf_op jit(solution)/shard_map/ppermute | solution.py:22
  264.7 6.1 %collective-permute-done.39 = f32[3,2,1,32]{3,2,1,0:T(1,128)S(1)} collective-permute-done((f32[3,2,1,32]{3,2,1,0:T(1,128)S(1)}, f32[3,2,1,32]{3,2,1,0:T(1,128)S(1)}, u32[]{:S(2)}, u32[]{:S(2)}) %collective-permute-start.39) | collective-permute-done | bytes 800 | tf_op jit(solution)/shard_map/ppermute | solution.py:33
  274.0 4.9 %collective-permute-start.44 = (f32[3,1,4,16]{3,2,0,1:T(4,128)S(1)}, f32[3,1,4,16]{3,2,0,1:T(4,128)S(1)}, u32[]{:S(2)}, u32[]{:S(2)}) collective-permute-start(f32[3,1,4,16]{3,2,0,1:T(4,128)S(1)} %fusion.198), channel_id=1, source_target_pairs={{0,1},{1,2},{2,3},{4,5},{5,6},{6,7},{8,9},{9,10},{10,11},{12,13},{... | collective-permute-start | bytes 2312 | tf_op jit(solution)/shard_map/ppermute | solution.py:22
  283.3 6.0 %collective-permute-done.47 = f32[3,1,1,16]{3,2,0,1:T(1,128)S(1)} collective-permute-done((f32[3,1,1,16]{3,2,0,1:T(1,128)S(1)}, f32[3,1,1,16]{3,2,0,1:T(1,128)S(1)}, u32[]{:S(2)}, u32[]{:S(2)}) %collective-permute-start.47) | collective-permute-done | bytes 224 | tf_op jit(solution)/shard_map/ppermute | solution.py:33
  291.5 4.3 %collective-permute-start.48 = (f32[3,1,4,16]{3,2,0,1:T(4,128)S(1)}, f32[3,1,4,16]{3,2,0,1:T(4,128)S(1)}, u32[]{:S(2)}, u32[]{:S(2)}) collective-permute-start(f32[3,1,4,16]{3,2,0,1:T(4,128)S(1)} %fusion.156), channel_id=1, source_target_pairs={{0,1},{1,2},{2,3},{4,5},{5,6},{6,7},{8,9},{9,10},{10,11},{12,13},{... | collective-permute-start | bytes 2312 | tf_op jit(solution)/shard_map/ppermute | solution.py:22
  300.2 6.0 %collective-permute-done.51 = f32[3,1,1,16]{3,2,0,1:T(1,128)S(1)} collective-permute-done((f32[3,1,1,16]{3,2,0,1:T(1,128)S(1)}, f32[3,1,1,16]{3,2,0,1:T(1,128)S(1)}, u32[]{:S(2)}, u32[]{:S(2)}) %collective-permute-start.51) | collective-permute-done | bytes 224 | tf_op jit(solution)/shard_map/ppermute | solution.py:33
  308.4 4.3 %collective-permute-start.52 = (f32[3,1,4,16]{3,2,0,1:T(4,128)S(1)}, f32[3,1,4,16]{3,2,0,1:T(4,128)S(1)}, u32[]{:S(2)}, u32[]{:S(2)}) collective-permute-start(f32[3,1,4,16]{3,2,0,1:T(4,128)S(1)} %fusion.166), channel_id=1, source_target_pairs={{0,1},{1,2},{2,3},{4,5},{5,6},{6,7},{8,9},{9,10},{10,11},{12,13},{... | collective-permute-start | bytes 2312 | tf_op jit(solution)/shard_map/ppermute | solution.py:22
  317.1 6.0 %collective-permute-done.55 = f32[3,1,1,16]{3,2,0,1:T(1,128)S(1)} collective-permute-done((f32[3,1,1,16]{3,2,0,1:T(1,128)S(1)}, f32[3,1,1,16]{3,2,0,1:T(1,128)S(1)}, u32[]{:S(2)}, u32[]{:S(2)}) %collective-permute-start.55) | collective-permute-done | bytes 224 | tf_op jit(solution)/shard_map/ppermute | solution.py:33
  325.3 4.3 %collective-permute-start.56 = (f32[3,1,4,16]{3,2,0,1:T(4,128)S(1)}, f32[3,1,4,16]{3,2,0,1:T(4,128)S(1)}, u32[]{:S(2)}, u32[]{:S(2)}) collective-permute-start(f32[3,1,4,16]{3,2,0,1:T(4,128)S(1)} %fusion.176), channel_id=1, source_target_pairs={{0,1},{1,2},{2,3},{4,5},{5,6},{6,7},{8,9},{9,10},{10,11},{12,13},{... | collective-permute-start | bytes 2312 | tf_op jit(solution)/shard_map/ppermute | solution.py:22
  334.0 6.0 %collective-permute-done.59 = f32[3,1,1,16]{3,2,0,1:T(1,128)S(1)} collective-permute-done((f32[3,1,1,16]{3,2,0,1:T(1,128)S(1)}, f32[3,1,1,16]{3,2,0,1:T(1,128)S(1)}, u32[]{:S(2)}, u32[]{:S(2)}) %collective-permute-start.59) | collective-permute-done | bytes 224 | tf_op jit(solution)/shard_map/ppermute | solution.py:33
  342.2 4.3 %collective-permute-start.60 = (f32[3,1,4,16]{3,2,0,1:T(4,128)S(1)}, f32[3,1,4,16]{3,2,0,1:T(4,128)S(1)}, u32[]{:S(2)}, u32[]{:S(2)}) collective-permute-start(f32[3,1,4,16]{3,2,0,1:T(4,128)S(1)} %fusion.186), channel_id=1, source_target_pairs={{0,1},{1,2},{2,3},{4,5},{5,6},{6,7},{8,9},{9,10},{10,11},{12,13},{... | collective-permute-start | bytes 2312 | tf_op jit(solution)/shard_map/ppermute | solution.py:22
  348.4 7.0 %collective-permute-start.62 = (f32[3,1,1,16]{3,2,0,1:T(1,128)S(1)}, f32[3,1,1,16]{3,2,0,1:T(1,128)S(1)}, u32[]{:S(2)}, u32[]{:S(2)}) collective-permute-start(f32[3,1,1,16]{3,2,0,1:T(1,128)S(1)} %get-tuple-element.176), channel_id=1, source_target_pairs={{0,4},{4,8},{8,12},{12,16},{16,20},{20,24},{24,28},{28,32},{32,36}... | collective-permute-start | bytes 584 | tf_op jit(solution)/shard_map/ppermute | solution.py:33
  357.2 3.4 collective-permute-start.64
  361.8 7.8 %collective-permute-start.66 = (f32[3,2,1,32]{3,2,1,0:T(1,128)S(1)}, f32[3,2,1,32]{3,2,1,0:T(1,128)S(1)}, u32[]{:S(2)}, u32[]{:S(2)}) collective-permute-start(f32[3,2,1,32]{3,2,1,0:T(1,128)S(1)} %get-tuple-element.140), channel_id=1, source_target_pairs={{0,4},{4,8},{8,12},{12,16},{16,20},{20,24},{24,28},{28,32},{32,36}... | collective-permute-start | bytes 2312 | tf_op jit(solution)/shard_map/ppermute | solution.py:33
  371.6 6.2 %collective-permute-done.67 = f32[3,2,1,32]{3,2,1,0:T(1,128)S(1)} collective-permute-done((f32[3,2,1,32]{3,2,1,0:T(1,128)S(1)}, f32[3,2,1,32]{3,2,1,0:T(1,128)S(1)}, u32[]{:S(2)}, u32[]{:S(2)}) %collective-permute-start.67) | collective-permute-done | bytes 800 | tf_op jit(solution)/shard_map/ppermute | solution.py:33
  380.4 4.3 %collective-permute-start.68 = (f32[3,1,16,64]{3,2,1,0:T(8,128)S(1)}, f32[3,1,16,64]{3,2,1,0:T(8,128)S(1)}, u32[]{:S(2)}, u32[]{:S(2)}) collective-permute-start(f32[3,1,16,64]{3,2,1,0:T(8,128)S(1)} %get-tuple-element.94), channel_id=1, source_target_pairs={{0,1},{1,2},{2,3},{4,5},{5,6},{6,7},{8,9},{9,10},{10,11},{12,13},{... | collective-permute-start | bytes 36872 | tf_op jit(solution)/shard_map/ppermute | solution.py:22
  390.4 6.1 %collective-permute-done.71 = f32[3,4,1,64]{3,2,1,0:T(1,128)S(1)} collective-permute-done((f32[3,4,1,64]{3,2,1,0:T(1,128)S(1)}, f32[3,4,1,64]{3,2,1,0:T(1,128)S(1)}, u32[]{:S(2)}, u32[]{:S(2)}) %collective-permute-start.71) | collective-permute-done | bytes 3104 | tf_op jit(solution)/shard_map/ppermute | solution.py:33
  399.2 4.3 %collective-permute-start.72 = (f32[3,1,32,128]{3,1,2,0:T(1,128)S(1)}, f32[3,1,32,128]{3,1,2,0:T(1,128)S(1)}, u32[]{:S(2)}, u32[]{:S(2)}) collective-permute-start(f32[3,1,32,128]{3,1,2,0:T(1,128)S(1)} %get-tuple-element.39), channel_id=1, source_target_pairs={{0,1},{1,2},{2,3},{4,5},{5,6},{6,7},{8,9},{9,10},{10,11},{12,13},{... | collective-permute-start | bytes 147464 | tf_op jit(solution)/shard_map/ppermute | solution.py:22
  409.1 6.2 %collective-permute-done.75 = f32[3,8,1,128]{3,1,2,0:T(8,128)S(1)} collective-permute-done((f32[3,8,1,128]{3,1,2,0:T(8,128)S(1)}, f32[3,8,1,128]{3,1,2,0:T(8,128)S(1)}, u32[]{:S(2)}, u32[]{:S(2)}) %collective-permute-start.75) | collective-permute-done | bytes 12320 | tf_op jit(solution)/shard_map/ppermute | solution.py:33
  (337 shorter events, 135.0 us)
Async XLA Ops:
  6.1 62.3 %collective-permute-start.7 = (f32[1,8,1,128]{3,1,2,0:T(8,128)S(1)}, f32[1,8,1,128]{3,1,2,0:T(8,128)S(1)}, u32[]{:S(2)}, u32[]{:S(2)}) collective-permute-start(f32[1,8,1,128]{3,1,2,0:T(8,128)S(1)} %get-tuple-element.80), channel_id=1, source_target_pairs={{4,0},{8,4},{12,8},{16,12},{20,16},{24,20},{28,24},{32,28},{36,32}... | collective-permute-start | bytes 12296 | tf_op jit(solution)/shard_map/ppermute | solution.py:33
  22.6 38.5 %collective-permute-start.17 = (f32[1,1,16,64]{3,2,1,0:T(8,128)S(1)}, f32[1,1,16,64]{3,2,1,0:T(8,128)S(1)}, u32[]{:S(2)}, u32[]{:S(2)}) collective-permute-start(f32[1,1,16,64]{3,2,1,0:T(8,128)S(1)} %get-tuple-element.126), channel_id=1, source_target_pairs={{1,0},{2,1},{3,2},{5,4},{6,5},{7,6},{9,8},{10,9},{11,10},{13,12},{... | collective-permute-start | bytes 12296 | tf_op jit(solution)/shard_map/ppermute | solution.py:25
  23.9 37.2 %collective-permute-start.16 = (f32[1,1,16,64]{3,2,1,0:T(8,128)S(1)}, f32[1,1,16,64]{3,2,1,0:T(8,128)S(1)}, u32[]{:S(2)}, u32[]{:S(2)}) collective-permute-start(f32[1,1,16,64]{3,2,1,0:T(8,128)S(1)} %get-tuple-element.125), channel_id=1, source_target_pairs={{0,1},{1,2},{2,3},{4,5},{5,6},{6,7},{8,9},{9,10},{10,11},{12,13},{... | collective-permute-start | bytes 12296 | tf_op jit(solution)/shard_map/ppermute | solution.py:22
  27.9 29.5 %collective-permute-start.19 = (f32[1,4,1,64]{3,2,1,0:T(1,128)S(1)}, f32[1,4,1,64]{3,2,1,0:T(1,128)S(1)}, u32[]{:S(2)}, u32[]{:S(2)}) collective-permute-start(f32[1,4,1,64]{3,2,1,0:T(1,128)S(1)} %get-tuple-element.130), channel_id=1, source_target_pairs={{4,0},{8,4},{12,8},{16,12},{20,16},{24,20},{28,24},{32,28},{36,32}... | collective-permute-start | bytes 3080 | tf_op jit(solution)/shard_map/ppermute | solution.py:33
  30.7 29.1 %collective-permute-start.18 = (f32[1,4,1,64]{3,1,2,0:T(4,128)S(1)}, f32[1,4,1,64]{3,1,2,0:T(4,128)S(1)}, u32[]{:S(2)}, u32[]{:S(2)}) collective-permute-start(f32[1,4,1,64]{3,1,2,0:T(4,128)S(1)} %bitcast.178), channel_id=1, source_target_pairs={{0,4},{4,8},{8,12},{12,16},{16,20},{20,24},{24,28},{28,32},{32,36}... | collective-permute-start | bytes 3080 | tf_op jit(solution)/shard_map/ppermute | solution.py:33
  57.5 13.7 %collective-permute-start.6 = (f32[1,8,1,128]{3,1,2,0:T(8,128)S(1)}, f32[1,8,1,128]{3,1,2,0:T(8,128)S(1)}, u32[]{:S(2)}, u32[]{:S(2)}) collective-permute-start(f32[1,8,1,128]{3,1,2,0:T(8,128)S(1)} %get-tuple-element.79), channel_id=1, source_target_pairs={{0,4},{4,8},{8,12},{12,16},{16,20},{20,24},{24,28},{28,32},{32,36}... | collective-permute-start | bytes 12296 | tf_op jit(solution)/shard_map/ppermute | solution.py:33
  59.8 41.7 %collective-permute-start.5 = (f32[1,1,32,128]{3,2,1,0:T(8,128)S(1)}, f32[1,1,32,128]{3,2,1,0:T(8,128)S(1)}, u32[]{:S(2)}, u32[]{:S(2)}) collective-permute-start(f32[1,1,32,128]{3,2,1,0:T(8,128)S(1)} %bitcast.169), channel_id=1, source_target_pairs={{1,0},{2,1},{3,2},{5,4},{6,5},{7,6},{9,8},{10,9},{11,10},{13,12},{... | collective-permute-start | bytes 49160 | tf_op jit(solution)/shard_map/ppermute | solution.py:25
  62.5 20.9 %collective-permute-start.28 = (f32[1,1,8,32]{3,2,1,0:T(8,128)S(1)}, f32[1,1,8,32]{3,2,1,0:T(8,128)S(1)}, u32[]{:S(2)}, u32[]{:S(2)}) collective-permute-start(f32[1,1,8,32]{3,2,1,0:T(8,128)S(1)} %get-tuple-element.166), channel_id=1, source_target_pairs={{0,1},{1,2},{2,3},{4,5},{5,6},{6,7},{8,9},{9,10},{10,11},{12,13},{... | collective-permute-start | bytes 3080 | tf_op jit(solution)/shard_map/ppermute | solution.py:22
  67.2 16.2 %collective-permute-start.29 = (f32[1,1,8,32]{3,2,1,0:T(8,128)S(1)}, f32[1,1,8,32]{3,2,1,0:T(8,128)S(1)}, u32[]{:S(2)}, u32[]{:S(2)}) collective-permute-start(f32[1,1,8,32]{3,2,1,0:T(8,128)S(1)} %get-tuple-element.169), channel_id=1, source_target_pairs={{1,0},{2,1},{3,2},{5,4},{6,5},{7,6},{9,8},{10,9},{11,10},{13,12},{... | collective-permute-start | bytes 3080 | tf_op jit(solution)/shard_map/ppermute | solution.py:25
  68.5 10.9 %collective-permute-start.31 = (f32[1,2,1,32]{3,2,1,0:T(1,128)S(1)}, f32[1,2,1,32]{3,2,1,0:T(1,128)S(1)}, u32[]{:S(2)}, u32[]{:S(2)}) collective-permute-start(f32[1,2,1,32]{3,2,1,0:T(1,128)S(1)} %get-tuple-element.171), channel_id=1, source_target_pairs={{4,0},{8,4},{12,8},{16,12},{20,16},{24,20},{28,24},{32,28},{36,32}... | collective-permute-start | bytes 776 | tf_op jit(solution)/shard_map/ppermute | solution.py:33
  71.1 12.2 %collective-permute-start.30 = (f32[1,2,1,32]{3,2,1,0:T(1,128)S(1)}, f32[1,2,1,32]{3,2,1,0:T(1,128)S(1)}, u32[]{:S(2)}, u32[]{:S(2)}) collective-permute-start(f32[1,2,1,32]{3,2,1,0:T(1,128)S(1)} %get-tuple-element.170), channel_id=1, source_target_pairs={{0,4},{4,8},{8,12},{12,16},{16,20},{20,24},{24,28},{28,32},{32,36}... | collective-permute-start | bytes 776 | tf_op jit(solution)/shard_map/ppermute | solution.py:33
  79.4 22.1 %collective-permute-start.4 = (f32[1,1,32,128]{3,2,1,0:T(8,128)S(1)}, f32[1,1,32,128]{3,2,1,0:T(8,128)S(1)}, u32[]{:S(2)}, u32[]{:S(2)}) collective-permute-start(f32[1,1,32,128]{3,2,1,0:T(8,128)S(1)} %bitcast.168), channel_id=1, source_target_pairs={{0,1},{1,2},{2,3},{4,5},{5,6},{6,7},{8,9},{9,10},{10,11},{12,13},{... | collective-permute-start | bytes 49160 | tf_op jit(solution)/shard_map/ppermute | solution.py:22
  84.2 14.1 %collective-permute-start.40 = (f32[1,1,4,16]{3,2,1,0:T(4,128)S(1)}, f32[1,1,4,16]{3,2,1,0:T(4,128)S(1)}, u32[]{:S(2)}, u32[]{:S(2)}) collective-permute-start(f32[1,1,4,16]{3,2,1,0:T(4,128)S(1)} %multiply_bitcast_fusion.4), channel_id=1, source_target_pairs={{0,1},{1,2},{2,3},{4,5},{5,6},{6,7},{8,9},{9,10},{10,11},{12,13},{... | collective-permute-start | bytes 776 | tf_op jit(solution)/shard_map/ppermute | solution.py:22
  87.5 8.9 %collective-permute-start.43 = (f32[1,1,1,16]{3,2,1,0:T(1,128)S(1)}, f32[1,1,1,16]{3,2,1,0:T(1,128)S(1)}, u32[]{:S(2)}, u32[]{:S(2)}) collective-permute-start(f32[1,1,1,16]{3,2,1,0:T(1,128)S(1)} %get-tuple-element.216), channel_id=1, source_target_pairs={{4,0},{8,4},{12,8},{16,12},{20,16},{24,20},{28,24},{32,28},{36,32}... | collective-permute-start | bytes 200 | tf_op jit(solution)/shard_map/ppermute | solution.py:33
  109.2 11.0 %collective-permute-start.2 = (f32[1,8,1,128]{3,1,2,0:T(8,128)S(1)}, f32[1,8,1,128]{3,1,2,0:T(8,128)S(1)}, u32[]{:S(2)}, u32[]{:S(2)}) collective-permute-start(f32[1,8,1,128]{3,1,2,0:T(8,128)S(1)} %get-tuple-element.72), channel_id=1, source_target_pairs={{0,4},{4,8},{8,12},{12,16},{16,20},{20,24},{24,28},{28,32},{32,36}... | collective-permute-start | bytes 12296 | tf_op jit(solution)/shard_map/ppermute | solution.py:33
  123.9 20.2 %collective-permute-start.8 = (f32[3,1,32,128]{3,1,2,0:T(1,128)S(1)}, f32[3,1,32,128]{3,1,2,0:T(1,128)S(1)}, u32[]{:S(2)}, u32[]{:S(2)}) collective-permute-start(f32[3,1,32,128]{3,1,2,0:T(1,128)S(1)} %get-tuple-element.59), channel_id=1, source_target_pairs={{0,1},{1,2},{2,3},{4,5},{5,6},{6,7},{8,9},{9,10},{10,11},{12,13},{... | collective-permute-start | bytes 147464 | tf_op jit(solution)/shard_map/ppermute | solution.py:22
  125.8 18.3 %collective-permute-start.9 = (f32[3,1,32,128]{3,1,2,0:T(1,128)S(1)}, f32[3,1,32,128]{3,1,2,0:T(1,128)S(1)}, u32[]{:S(2)}, u32[]{:S(2)}) collective-permute-start(f32[3,1,32,128]{3,1,2,0:T(1,128)S(1)} %get-tuple-element.58), channel_id=1, source_target_pairs={{1,0},{2,1},{3,2},{5,4},{6,5},{7,6},{9,8},{10,9},{11,10},{13,12},{... | collective-permute-start | bytes 147464 | tf_op jit(solution)/shard_map/ppermute | solution.py:25
  127.1 10.7 %collective-permute-start.10 = (f32[3,8,1,128]{3,1,2,0:T(8,128)S(1)}, f32[3,8,1,128]{3,1,2,0:T(8,128)S(1)}, u32[]{:S(2)}, u32[]{:S(2)}) collective-permute-start(f32[3,8,1,128]{3,1,2,0:T(8,128)S(1)} %get-tuple-element.55), channel_id=1, source_target_pairs={{0,4},{4,8},{8,12},{12,16},{16,20},{20,24},{24,28},{28,32},{32,36}... | collective-permute-start | bytes 36872 | tf_op jit(solution)/shard_map/ppermute | solution.py:33
  135.8 8.3 %collective-permute-start.11 = (f32[3,8,1,128]{3,1,2,0:T(8,128)S(1)}, f32[3,8,1,128]{3,1,2,0:T(8,128)S(1)}, u32[]{:S(2)}, u32[]{:S(2)}) collective-permute-start(f32[3,8,1,128]{3,1,2,0:T(8,128)S(1)} %get-tuple-element.54), channel_id=1, source_target_pairs={{4,0},{8,4},{12,8},{16,12},{20,16},{24,20},{28,24},{32,28},{36,32}... | collective-permute-start | bytes 36872 | tf_op jit(solution)/shard_map/ppermute | solution.py:33
  145.2 16.1 %collective-permute-start.12 = (f32[3,1,32,128]{3,1,2,0:T(1,128)S(1)}, f32[3,1,32,128]{3,1,2,0:T(1,128)S(1)}, u32[]{:S(2)}, u32[]{:S(2)}) collective-permute-start(f32[3,1,32,128]{3,1,2,0:T(1,128)S(1)} %get-tuple-element.49), channel_id=1, source_target_pairs={{0,1},{1,2},{2,3},{4,5},{5,6},{6,7},{8,9},{9,10},{10,11},{12,13},{... | collective-permute-start | bytes 147464 | tf_op jit(solution)/shard_map/ppermute | solution.py:22
  149.5 11.9 %collective-permute-start.13 = (f32[3,1,32,128]{3,1,2,0:T(1,128)S(1)}, f32[3,1,32,128]{3,1,2,0:T(1,128)S(1)}, u32[]{:S(2)}, u32[]{:S(2)}) collective-permute-start(f32[3,1,32,128]{3,1,2,0:T(1,128)S(1)} %get-tuple-element.48), channel_id=1, source_target_pairs={{1,0},{2,1},{3,2},{5,4},{6,5},{7,6},{9,8},{10,9},{11,10},{13,12},{... | collective-permute-start | bytes 147464 | tf_op jit(solution)/shard_map/ppermute | solution.py:25
  153.0 8.3 %collective-permute-start.15 = (f32[3,8,1,128]{3,1,2,0:T(8,128)S(1)}, f32[3,8,1,128]{3,1,2,0:T(8,128)S(1)}, u32[]{:S(2)}, u32[]{:S(2)}) collective-permute-start(f32[3,8,1,128]{3,1,2,0:T(8,128)S(1)} %get-tuple-element.44), channel_id=1, source_target_pairs={{4,0},{8,4},{12,8},{16,12},{20,16},{24,20},{28,24},{32,28},{36,32}... | collective-permute-start | bytes 36872 | tf_op jit(solution)/shard_map/ppermute | solution.py:33
  198.3 16.1 %collective-permute-start.20 = (f32[3,1,16,64]{3,2,1,0:T(8,128)S(1)}, f32[3,1,16,64]{3,2,1,0:T(8,128)S(1)}, u32[]{:S(2)}, u32[]{:S(2)}) collective-permute-start(f32[3,1,16,64]{3,2,1,0:T(8,128)S(1)} %get-tuple-element.114), channel_id=1, source_target_pairs={{0,1},{1,2},{2,3},{4,5},{5,6},{6,7},{8,9},{9,10},{10,11},{12,13},{... | collective-permute-start | bytes 36872 | tf_op jit(solution)/shard_map/ppermute | solution.py:22
  202.5 11.8 %collective-permute-start.21 = (f32[3,1,16,64]{3,2,1,0:T(8,128)S(1)}, f32[3,1,16,64]{3,2,1,0:T(8,128)S(1)}, u32[]{:S(2)}, u32[]{:S(2)}) collective-permute-start(f32[3,1,16,64]{3,2,1,0:T(8,128)S(1)} %get-tuple-element.113), channel_id=1, source_target_pairs={{1,0},{2,1},{3,2},{5,4},{6,5},{7,6},{9,8},{10,9},{11,10},{13,12},{... | collective-permute-start | bytes 36872 | tf_op jit(solution)/shard_map/ppermute | solution.py:25
  214.7 16.1 %collective-permute-start.24 = (f32[3,1,16,64]{3,2,1,0:T(8,128)S(1)}, f32[3,1,16,64]{3,2,1,0:T(8,128)S(1)}, u32[]{:S(2)}, u32[]{:S(2)}) collective-permute-start(f32[3,1,16,64]{3,2,1,0:T(8,128)S(1)} %get-tuple-element.104), channel_id=1, source_target_pairs={{0,1},{1,2},{2,3},{4,5},{5,6},{6,7},{8,9},{9,10},{10,11},{12,13},{... | collective-permute-start | bytes 36872 | tf_op jit(solution)/shard_map/ppermute | solution.py:22
  219.0 11.8 %collective-permute-start.25 = (f32[3,1,16,64]{3,2,1,0:T(8,128)S(1)}, f32[3,1,16,64]{3,2,1,0:T(8,128)S(1)}, u32[]{:S(2)}, u32[]{:S(2)}) collective-permute-start(f32[3,1,16,64]{3,2,1,0:T(8,128)S(1)} %get-tuple-element.103), channel_id=1, source_target_pairs={{1,0},{2,1},{3,2},{5,4},{6,5},{7,6},{9,8},{10,9},{11,10},{13,12},{... | collective-permute-start | bytes 36872 | tf_op jit(solution)/shard_map/ppermute | solution.py:25
  237.6 16.0 %collective-permute-start.32 = (f32[3,1,8,32]{3,2,1,0:T(8,128)S(1)}, f32[3,1,8,32]{3,2,1,0:T(8,128)S(1)}, u32[]{:S(2)}, u32[]{:S(2)}) collective-permute-start(f32[3,1,8,32]{3,2,1,0:T(8,128)S(1)} %get-tuple-element.157), channel_id=1, source_target_pairs={{0,1},{1,2},{2,3},{4,5},{5,6},{6,7},{8,9},{9,10},{10,11},{12,13},{... | collective-permute-start | bytes 9224 | tf_op jit(solution)/shard_map/ppermute | solution.py:22
  241.9 11.8 %collective-permute-start.33 = (f32[3,1,8,32]{3,2,1,0:T(8,128)S(1)}, f32[3,1,8,32]{3,2,1,0:T(8,128)S(1)}, u32[]{:S(2)}, u32[]{:S(2)}) collective-permute-start(f32[3,1,8,32]{3,2,1,0:T(8,128)S(1)} %get-tuple-element.158), channel_id=1, source_target_pairs={{1,0},{2,1},{3,2},{5,4},{6,5},{7,6},{9,8},{10,9},{11,10},{13,12},{... | collective-permute-start | bytes 9224 | tf_op jit(solution)/shard_map/ppermute | solution.py:25
  254.7 16.1 %collective-permute-start.36 = (f32[3,1,8,32]{3,2,1,0:T(8,128)S(1)}, f32[3,1,8,32]{3,2,1,0:T(8,128)S(1)}, u32[]{:S(2)}, u32[]{:S(2)}) collective-permute-start(f32[3,1,8,32]{3,2,1,0:T(8,128)S(1)} %get-tuple-element.149), channel_id=1, source_target_pairs={{0,1},{1,2},{2,3},{4,5},{5,6},{6,7},{8,9},{9,10},{10,11},{12,13},{... | collective-permute-start | bytes 9224 | tf_op jit(solution)/shard_map/ppermute | solution.py:22
  258.9 11.8 %collective-permute-start.37 = (f32[3,1,8,32]{3,2,1,0:T(8,128)S(1)}, f32[3,1,8,32]{3,2,1,0:T(8,128)S(1)}, u32[]{:S(2)}, u32[]{:S(2)}) collective-permute-start(f32[3,1,8,32]{3,2,1,0:T(8,128)S(1)} %get-tuple-element.150), channel_id=1, source_target_pairs={{1,0},{2,1},{3,2},{5,4},{6,5},{7,6},{9,8},{10,9},{11,10},{13,12},{... | collective-permute-start | bytes 9224 | tf_op jit(solution)/shard_map/ppermute | solution.py:25
  272.7 16.7 %collective-permute-start.45 = (f32[3,1,4,16]{3,2,0,1:T(4,128)S(1)}, f32[3,1,4,16]{3,2,0,1:T(4,128)S(1)}, u32[]{:S(2)}, u32[]{:S(2)}) collective-permute-start(f32[3,1,4,16]{3,2,0,1:T(4,128)S(1)} %fusion.198), channel_id=1, source_target_pairs={{1,0},{2,1},{3,2},{5,4},{6,5},{7,6},{9,8},{10,9},{11,10},{13,12},{... | collective-permute-start | bytes 2312 | tf_op jit(solution)/shard_map/ppermute | solution.py:25
  274.0 15.4 %collective-permute-start.44 = (f32[3,1,4,16]{3,2,0,1:T(4,128)S(1)}, f32[3,1,4,16]{3,2,0,1:T(4,128)S(1)}, u32[]{:S(2)}, u32[]{:S(2)}) collective-permute-start(f32[3,1,4,16]{3,2,0,1:T(4,128)S(1)} %fusion.198), channel_id=1, source_target_pairs={{0,1},{1,2},{2,3},{4,5},{5,6},{6,7},{8,9},{9,10},{10,11},{12,13},{... | collective-permute-start | bytes 2312 | tf_op jit(solution)/shard_map/ppermute | solution.py:22
  290.2 16.0 %collective-permute-start.49 = (f32[3,1,4,16]{3,2,0,1:T(4,128)S(1)}, f32[3,1,4,16]{3,2,0,1:T(4,128)S(1)}, u32[]{:S(2)}, u32[]{:S(2)}) collective-permute-start(f32[3,1,4,16]{3,2,0,1:T(4,128)S(1)} %fusion.156), channel_id=1, source_target_pairs={{1,0},{2,1},{3,2},{5,4},{6,5},{7,6},{9,8},{10,9},{11,10},{13,12},{... | collective-permute-start | bytes 2312 | tf_op jit(solution)/shard_map/ppermute | solution.py:25
  291.5 14.7 %collective-permute-start.48 = (f32[3,1,4,16]{3,2,0,1:T(4,128)S(1)}, f32[3,1,4,16]{3,2,0,1:T(4,128)S(1)}, u32[]{:S(2)}, u32[]{:S(2)}) collective-permute-start(f32[3,1,4,16]{3,2,0,1:T(4,128)S(1)} %fusion.156), channel_id=1, source_target_pairs={{0,1},{1,2},{2,3},{4,5},{5,6},{6,7},{8,9},{9,10},{10,11},{12,13},{... | collective-permute-start | bytes 2312 | tf_op jit(solution)/shard_map/ppermute | solution.py:22
  307.1 16.0 %collective-permute-start.53 = (f32[3,1,4,16]{3,2,0,1:T(4,128)S(1)}, f32[3,1,4,16]{3,2,0,1:T(4,128)S(1)}, u32[]{:S(2)}, u32[]{:S(2)}) collective-permute-start(f32[3,1,4,16]{3,2,0,1:T(4,128)S(1)} %fusion.166), channel_id=1, source_target_pairs={{1,0},{2,1},{3,2},{5,4},{6,5},{7,6},{9,8},{10,9},{11,10},{13,12},{... | collective-permute-start | bytes 2312 | tf_op jit(solution)/shard_map/ppermute | solution.py:25
  308.4 14.7 %collective-permute-start.52 = (f32[3,1,4,16]{3,2,0,1:T(4,128)S(1)}, f32[3,1,4,16]{3,2,0,1:T(4,128)S(1)}, u32[]{:S(2)}, u32[]{:S(2)}) collective-permute-start(f32[3,1,4,16]{3,2,0,1:T(4,128)S(1)} %fusion.166), channel_id=1, source_target_pairs={{0,1},{1,2},{2,3},{4,5},{5,6},{6,7},{8,9},{9,10},{10,11},{12,13},{... | collective-permute-start | bytes 2312 | tf_op jit(solution)/shard_map/ppermute | solution.py:22
  324.0 16.0 %collective-permute-start.57 = (f32[3,1,4,16]{3,2,0,1:T(4,128)S(1)}, f32[3,1,4,16]{3,2,0,1:T(4,128)S(1)}, u32[]{:S(2)}, u32[]{:S(2)}) collective-permute-start(f32[3,1,4,16]{3,2,0,1:T(4,128)S(1)} %fusion.176), channel_id=1, source_target_pairs={{1,0},{2,1},{3,2},{5,4},{6,5},{7,6},{9,8},{10,9},{11,10},{13,12},{... | collective-permute-start | bytes 2312 | tf_op jit(solution)/shard_map/ppermute | solution.py:25
  325.3 14.7 %collective-permute-start.56 = (f32[3,1,4,16]{3,2,0,1:T(4,128)S(1)}, f32[3,1,4,16]{3,2,0,1:T(4,128)S(1)}, u32[]{:S(2)}, u32[]{:S(2)}) collective-permute-start(f32[3,1,4,16]{3,2,0,1:T(4,128)S(1)} %fusion.176), channel_id=1, source_target_pairs={{0,1},{1,2},{2,3},{4,5},{5,6},{6,7},{8,9},{9,10},{10,11},{12,13},{... | collective-permute-start | bytes 2312 | tf_op jit(solution)/shard_map/ppermute | solution.py:22
  340.9 15.2 %collective-permute-start.61 = (f32[3,1,4,16]{3,2,0,1:T(4,128)S(1)}, f32[3,1,4,16]{3,2,0,1:T(4,128)S(1)}, u32[]{:S(2)}, u32[]{:S(2)}) collective-permute-start(f32[3,1,4,16]{3,2,0,1:T(4,128)S(1)} %fusion.186), channel_id=1, source_target_pairs={{1,0},{2,1},{3,2},{5,4},{6,5},{7,6},{9,8},{10,9},{11,10},{13,12},{... | collective-permute-start | bytes 2312 | tf_op jit(solution)/shard_map/ppermute | solution.py:25
  342.2 13.9 %collective-permute-start.60 = (f32[3,1,4,16]{3,2,0,1:T(4,128)S(1)}, f32[3,1,4,16]{3,2,0,1:T(4,128)S(1)}, u32[]{:S(2)}, u32[]{:S(2)}) collective-permute-start(f32[3,1,4,16]{3,2,0,1:T(4,128)S(1)} %fusion.186), channel_id=1, source_target_pairs={{0,1},{1,2},{2,3},{4,5},{5,6},{6,7},{8,9},{9,10},{10,11},{12,13},{... | collective-permute-start | bytes 2312 | tf_op jit(solution)/shard_map/ppermute | solution.py:22
  346.5 8.9 %collective-permute-start.63 = (f32[3,1,1,16]{3,2,0,1:T(1,128)S(1)}, f32[3,1,1,16]{3,2,0,1:T(1,128)S(1)}, u32[]{:S(2)}, u32[]{:S(2)}) collective-permute-start(f32[3,1,1,16]{3,2,0,1:T(1,128)S(1)} %get-tuple-element.177), channel_id=1, source_target_pairs={{4,0},{8,4},{12,8},{16,12},{20,16},{24,20},{28,24},{32,28},{36,32}... | collective-permute-start | bytes 584 | tf_op jit(solution)/shard_map/ppermute | solution.py:33
  357.2 20.7 %collective-permute-start.64 = (f32[3,1,8,32]{3,2,1,0:T(8,128)S(1)}, f32[3,1,8,32]{3,2,1,0:T(8,128)S(1)}, u32[]{:S(2)}, u32[]{:S(2)}) collective-permute-start(f32[3,1,8,32]{3,2,1,0:T(8,128)S(1)} %get-tuple-element.141), channel_id=1, source_target_pairs={{0,1},{1,2},{2,3},{4,5},{5,6},{6,7},{8,9},{9,10},{10,11},{12,13},{... | collective-permute-start | bytes 9224 | tf_op jit(solution)/shard_map/ppermute | solution.py:22
  360.5 17.3 %collective-permute-start.65 = (f32[3,1,8,32]{3,2,1,0:T(8,128)S(1)}, f32[3,1,8,32]{3,2,1,0:T(8,128)S(1)}, u32[]{:S(2)}, u32[]{:S(2)}) collective-permute-start(f32[3,1,8,32]{3,2,1,0:T(8,128)S(1)} %get-tuple-element.142), channel_id=1, source_target_pairs={{1,0},{2,1},{3,2},{5,4},{6,5},{7,6},{9,8},{10,9},{11,10},{13,12},{... | collective-permute-start | bytes 9224 | tf_op jit(solution)/shard_map/ppermute | solution.py:25
  361.8 9.8 %collective-permute-start.66 = (f32[3,2,1,32]{3,2,1,0:T(1,128)S(1)}, f32[3,2,1,32]{3,2,1,0:T(1,128)S(1)}, u32[]{:S(2)}, u32[]{:S(2)}) collective-permute-start(f32[3,2,1,32]{3,2,1,0:T(1,128)S(1)} %get-tuple-element.140), channel_id=1, source_target_pairs={{0,4},{4,8},{8,12},{12,16},{16,20},{20,24},{24,28},{28,32},{32,36}... | collective-permute-start | bytes 2312 | tf_op jit(solution)/shard_map/ppermute | solution.py:33
  380.4 16.1 %collective-permute-start.68 = (f32[3,1,16,64]{3,2,1,0:T(8,128)S(1)}, f32[3,1,16,64]{3,2,1,0:T(8,128)S(1)}, u32[]{:S(2)}, u32[]{:S(2)}) collective-permute-start(f32[3,1,16,64]{3,2,1,0:T(8,128)S(1)} %get-tuple-element.94), channel_id=1, source_target_pairs={{0,1},{1,2},{2,3},{4,5},{5,6},{6,7},{8,9},{9,10},{10,11},{12,13},{... | collective-permute-start | bytes 36872 | tf_op jit(solution)/shard_map/ppermute | solution.py:22
  384.7 11.8 %collective-permute-start.69 = (f32[3,1,16,64]{3,2,1,0:T(8,128)S(1)}, f32[3,1,16,64]{3,2,1,0:T(8,128)S(1)}, u32[]{:S(2)}, u32[]{:S(2)}) collective-permute-start(f32[3,1,16,64]{3,2,1,0:T(8,128)S(1)} %get-tuple-element.93), channel_id=1, source_target_pairs={{1,0},{2,1},{3,2},{5,4},{6,5},{7,6},{9,8},{10,9},{11,10},{13,12},{... | collective-permute-start | bytes 36872 | tf_op jit(solution)/shard_map/ppermute | solution.py:25
  399.2 16.1 %collective-permute-start.72 = (f32[3,1,32,128]{3,1,2,0:T(1,128)S(1)}, f32[3,1,32,128]{3,1,2,0:T(1,128)S(1)}, u32[]{:S(2)}, u32[]{:S(2)}) collective-permute-start(f32[3,1,32,128]{3,1,2,0:T(1,128)S(1)} %get-tuple-element.39), channel_id=1, source_target_pairs={{0,1},{1,2},{2,3},{4,5},{5,6},{6,7},{8,9},{9,10},{10,11},{12,13},{... | collective-permute-start | bytes 147464 | tf_op jit(solution)/shard_map/ppermute | solution.py:22
  403.4 11.9 %collective-permute-start.73 = (f32[3,1,32,128]{3,1,2,0:T(1,128)S(1)}, f32[3,1,32,128]{3,1,2,0:T(1,128)S(1)}, u32[]{:S(2)}, u32[]{:S(2)}) collective-permute-start(f32[3,1,32,128]{3,1,2,0:T(1,128)S(1)} %get-tuple-element.38), channel_id=1, source_target_pairs={{1,0},{2,1},{3,2},{5,4},{6,5},{7,6},{9,8},{10,9},{11,10},{13,12},{... | collective-permute-start | bytes 147464 | tf_op jit(solution)/shard_map/ppermute | solution.py:25
  (63 other events, 3409.6 us)
where the time goes:
time: 422 us; the launch traced here: 418 us
  starting transfers between devices  215 us (51%)
  waiting for transfers between devices  85.6 us (20%)
  local copies, waits for them, and re-layouts  61.4 us (15%)
  other arithmetic  54.1 us (13%)
    ppermute x38, starting transfers between devices, passed_along(): return lax.ppermute(x, axis, pairs)  115 us
    ppermute x38, waiting for transfers between devices, passed_along(): return lax.ppermute(x, axis, pairs)  81.8 us
    ppermute x19, starting transfers between devices, with_halo(): lax.ppermute(lax.slice_in_dim(block, block.shape[dim] - width, None, axis...  75.5 us
    reshape x5, local copies, waits for them, and re-layouts, block_sum(): field.reshape(dims_now[0], dims_now[1] // 2, 2, dims_now[2] // 2, 2, dims...  51.2 us
    ppermute x19, starting transfers between devices, with_halo(): lax.ppermute(lax.slice_in_dim(block, 0, width, axis=dim), axis, backward)  24.5 us
    reduce_sum x13, other arithmetic, block_sum(): return shaped.sum(axis=(2, 4, 6))  20.8 us
    add x5, other arithmetic, coefficients(): low_face + high_face  10.8 us
  transfers between devices with their start and end apart: 76, of which 17 were waited for; matrix products, arithmetic and copies ran while one was open for 10% of the time, Pallas kernels for 0%

commit v1 on v0

v1 whole, which is shorter than its diff:
```python
import functools

import jax
import jax.numpy as jnp
from jax import lax
from jax.experimental import pallas as pl
from jax.experimental.pallas import tpu as pltpu
from jax.sharding import PartitionSpec as P

PENALTY = 50.0
OMEGA = 0.6
KEEP = 1.0 - OMEGA
F32 = jnp.float32
HI = lax.Precision.HIGHEST
NEAR = tuple((dt, dh) for dt in (-1, 0, 1) for dh in (-1, 0, 1) if (dt, dh) != (0, 0))
FAR = tuple((dt, k) for dt in (-2, -1, 0, 1, 2) for k in (0, 1, 2, 3) if (dt, k) != (0, 0))


def iota(shape, axis):
    return lax.broadcasted_iota(jnp.int32, shape, axis)


def one_hot(shape, cond):
    return jnp.where(cond(iota(shape, 0), iota(shape, 1)), 1.0, 0.0).astype(F32)


def dot(a, b):
    return jnp.dot(a, b, preferred_element_type=F32, precision=HI)


def kernel(
    heights,
    tiles,
    mat_hbm,
    clamp_hbm,
    table,
    eigen,
    out,
    mat,
    cl,
    m_lo, m_hi, m_side, m_corner, m_stage,
    q1, q1_vert, q1_side, q1_stage,
    q2, q2_own,
    b1_vert, b1_side, b1_stage,
    b2, b2_own,
    S, SG, HZ, HR, HC, BB, WH, DD, V0, V1, RS,
    S1, HZ1, HR1, HC1, BB1, WH1, DD1, VA1, VB1, RS1, PO1,
    HZ2, HR2, HC2, WH2, DD2, VA2, VB2, PO2, T1,
    S3, HZ3, HR3, HC3, WH3, BB3, V3,
    T0, R4,
    local_sem,
    m_send, m_recv, q1_send, q1_recv, q2_send, q2_recv, b1_send, b1_recv, b2_send, b2_recv,
):
    i = lax.axis_index("tile")
    h = lax.axis_index("height")

    in_mat = pltpu.make_async_copy(mat_hbm, mat, local_sem.at[0])
    in_cl = pltpu.make_async_copy(clamp_hbm.at[pl.ds(0, 2)], cl, local_sem.at[1])
    in_mat.start()
    in_cl.start()

    def tile_ok(dt):
        return jnp.logical_and(i + dt >= 0, i + dt < tiles)

    def near_ok(dt, dh):
        return jnp.logical_and(tile_ok(dt), jnp.logical_and(h + dh >= 0, h + dh < heights))

    def far_id(dt, k):
        return {"tile": i + dt, "height": lax.rem(h + k, heights)}

    barrier = pltpu.get_barrier_semaphore()
    for dt, k in FAR:
        @pl.when(tile_ok(dt))
        def _():
            pl.semaphore_signal(
                barrier, inc=1, device_id=far_id(dt, k), device_id_type=pl.DeviceIdType.MESH
            )
    reach = sum(tile_ok(dt).astype(jnp.int32) for dt in (-2, -1, 0, 1, 2))

    in_mat.wait()
    in_cl.wait()
    for z in range(8):
        m_stage[0, z] = mat[z, 0:4]
        m_stage[1, z] = mat[z, 28:32]
    for z in range(2):
        m_stage[0, 8 + z] = cl[z, 0:4]
        m_stage[1, 8 + z] = cl[z, 28:32]

    pl.semaphore_wait(barrier, 4 * reach - 1)

    def near_copies(send, recv, refs):
        copies = []
        for k, (dt, dh) in enumerate(NEAR):
            src, dst = refs(dt, dh)
            copy = pltpu.make_async_remote_copy(
                src_ref=src, dst_ref=dst, send_sem=send.at[k], recv_sem=recv.at[k],
                device_id={"tile": i + dt, "height": h + dh},
                device_id_type=pl.DeviceIdType.MESH,
            )
            copies.append((copy, near_ok(dt, dh), near_ok(-dt, -dh)))
        return copies

    def far_copies(send, recv, own, field):
        copies = []
        for k, (dt, dh) in enumerate(FAR):
            copy = pltpu.make_async_remote_copy(
                src_ref=own,
                dst_ref=field.at[pl.ds(2 * h, 2), pl.ds(8 * (2 - dt), 8)],
                send_sem=send.at[k], recv_sem=recv.at[k],
                device_id=far_id(dt, dh), device_id_type=pl.DeviceIdType.MESH,
            )
            copies.append((copy, tile_ok(dt), tile_ok(-dt)))
        return copies

    def start(copies):
        for copy, sends, _ in copies:
            @pl.when(sends)
            def _():
                copy.start()

    def wait_recv(copies):
        for copy, _, receives in copies:
            @pl.when(receives)
            def _():
                copy.wait_recv()

    def wait_send(copies):
        for copy, sends, _ in copies:
            @pl.when(sends)
            def _():
                copy.wait_send()

    def label_refs(dt, dh):
        if dt == 0:
            return (mat.at[pl.ds(5, 3)], m_lo) if dh > 0 else (mat.at[pl.ds(0, 3)], m_hi)
        side = 0 if dt < 0 else 1
        if dh == 0:
            return m_stage.at[side], m_side.at[side]
        first = 6 if dh > 0 else 0
        return m_stage.at[side, pl.ds(first, 2)], m_corner.at[side, 0 if dh < 0 else 1]

    label_moves = near_copies(m_send, m_recv, label_refs)
    start(label_moves)

    st = [table[n] for n in range(3)]
    stress = [[table[n] * eigen[n, c] for c in range(3)] for n in range(3)]

    def look(m, values):
        return jnp.where(
            m == 0, values[0], jnp.where(m == 1, values[1], jnp.where(m == 2, values[2], 0.0))
        )

    take_lo = one_hot((128, 128), lambda l, j: jnp.logical_and(j < 64, l // 2 == j))
    take_hi = one_hot((128, 128), lambda l, j: l // 2 == j - 64)
    lowest = jnp.where(h == 0, 1.0, 0.0).astype(F32)

    for z in range(4):
        R4[0, z] = look(mat[2 * z], st) + look(mat[2 * z + 1], st)
    R4[1, 0] = (cl[0] + cl[1]).astype(F32)
    s_rows = jnp.concatenate(
        [R4[0, z, pl.ds(0, 16, 2)] + R4[0, z, pl.ds(1, 16, 2)] for z in range(4)], axis=0
    )
    p_rows = R4[1, 0, pl.ds(0, 16, 2)] + R4[1, 0, pl.ds(1, 16, 2)]
    s_one = dot(0.5 * s_rows, take_lo).reshape(4, 16, 128)
    p_one = dot((2.0 * PENALTY * lowest) * p_rows, take_hi)
    q1[0] = s_one[0] + p_one
    for z in range(1, 4):
        q1[z] = s_one[z]
    for z in range(4):
        q1_stage[0, z] = q1[z, 0:4]
        q1_stage[1, z] = q1[z, 12:16]

    def q1_refs(dt, dh):
        if dt == 0:
            return q1, q1_vert.at[0 if dh > 0 else 1]
        side = 0 if dt < 0 else 1
        return q1_stage.at[side], q1_side.at[side, dh + 1]

    q1_moves = near_copies(q1_send, q1_recv, q1_refs)
    start(q1_moves)

    for z in range(2):
        R4[1, z, 0:16] = q1[2 * z] + q1[2 * z + 1]
    q_rows = jnp.concatenate(
        [R4[1, z, pl.ds(0, 8, 2)] + R4[1, z, pl.ds(1, 8, 2)] for z in range(2)], axis=0
    )
    l, j = iota((128, 128), 0), iota((128, 128), 1)
    down_q = jnp.where(
        jnp.logical_and(j < 96, jnp.logical_and(l < 64, l // 2 == j % 32)), 0.5,
        jnp.where(jnp.logical_and(j >= 96, l // 2 == j - 64), 1.0, 0.0),
    ).astype(F32)
    q2_own[...] = dot(q_rows, down_q).reshape(2, 8, 128)
    q2_moves = far_copies(q2_send, q2_recv, q2_own, q2)
    start(q2_moves)
    q2[pl.ds(2 * h, 2), 16:24] = q2_own[...]

    lane = iota((40, 128), 1)
    sub8 = iota((8, 128), 0)
    wait_recv(label_moves)
    below, above = h > 0, h < heights - 1
    before, after = i > 0, i < tiles - 1

    def side_rows(z, ref_of):
        lo_ok, lo = ref_of(1)
        hi_ok, hi = ref_of(0)
        return jnp.concatenate([jnp.where(hi_ok, hi, -1), jnp.where(lo_ok, lo, -1)], axis=0)

    def labels(z):
        if z < 0:
            centre = jnp.where(below, m_lo[z + 3], -1)
            if z < -2:
                return jnp.concatenate([centre, jnp.full((8, 128), -1, jnp.int32)], axis=0)
            sides = side_rows(
                z, lambda s: (jnp.logical_and(below, before if s else after), m_corner[s, 1, z + 2])
            )
        elif z < 8:
            centre = mat[z]
            sides = side_rows(z, lambda s: (before if s else after, m_side[s, z]))
        else:
            centre = jnp.where(above, m_hi[z - 8], -1)
            if z > 9:
                return jnp.concatenate([centre, jnp.full((8, 128), -1, jnp.int32)], axis=0)
            sides = side_rows(
                z, lambda s: (jnp.logical_and(above, before if s else after), m_corner[s, 0, z - 8])
            )
        return jnp.concatenate([centre, sides], axis=0)

    for z in range(-3, 11):
        m = labels(z)
        S[z + 3] = look(m, st)
        for c in range(3):
            SG[c, z + 3] = look(m, [stress[n][c] for n in range(3)])
    for z in range(-3, 10):
        HZ[z + 3] = S[z + 3] + S[z + 4]

    def spring0(z):
        sides = jnp.concatenate(
            [jnp.where(after, m_side[0, 8 + z], 0), jnp.where(before, m_side[1, 8 + z], 0)], axis=0
        )
        return (2.0 * PENALTY * lowest) * jnp.concatenate([cl[z], sides], axis=0).astype(F32)

    for z in range(-2, 10):
        s = S[z + 3]
        s_r = pltpu.roll(s, 39, 0)
        s_c = jnp.where(lane < 127, pltpu.roll(s, 127, 1), 0.0)
        h_ru = s + s_r
        h_rl = pltpu.roll(h_ru, 1, 0)
        f_cu = s + s_c
        f_cl = s + jnp.where(lane > 0, pltpu.roll(s, 1, 1), 0.0)
        HR[0, z + 2] = h_rl
        HR[1, z + 2] = h_ru
        HC[0, z + 2] = jnp.where(lane > 0, f_cl, 0.0)
        HC[1, z + 2] = jnp.where(lane < 127, f_cu, 0.0)
        f = [HZ[z + 2] + HZ[z + 3], h_rl + h_ru, f_cl + f_cu]
        total = f[0] + f[1] + f[2]
        if 0 <= z < 2:
            total = total + spring0(z)
        g0 = SG[0, z + 2] - SG[0, z + 4]
        x = SG[1, z + 3]
        g1 = pltpu.roll(x, 1, 0) - pltpu.roll(x, 39, 0)
        x = SG[2, z + 3]
        g2 = jnp.where(lane > 0, pltpu.roll(x, 1, 1), 0.0) - jnp.where(
            lane < 127, pltpu.roll(x, 127, 1), 0.0
        )
        for c, g in enumerate((g0, g1, g2)):
            d = total + f[c]
            w = jnp.where(s > 0.0, OMEGA / jnp.where(s > 0.0, d, 1.0), 0.0)
            BB[c, z + 2] = g
            WH[c, z + 2] = w
            if 0 <= z < 8:
                DD[c, z] = d
            V0[c, z + 2] = w * g

    def apply0(v, off, c, z):
        x = v[c, z + off]
        a = HZ[z + 2] * v[c, z + off - 1] + HZ[z + 3] * v[c, z + off + 1]
        b = HR[0, z + 2] * pltpu.roll(x, 1, 0) + HR[1, z + 2] * pltpu.roll(x, 39, 0)
        e = HC[0, z + 2] * pltpu.roll(x, 1, 1) + HC[1, z + 2] * pltpu.roll(x, 127, 1)
        return x, (a + b + e) + (a, b, e)[c]

    for z in range(-1, 9):
        for c in range(3):
            x, n = apply0(V0, 2, c, z)
            V1[c, z + 1] = KEEP * x + WH[c, z + 2] * (BB[c, z + 2] + n)

    for z in range(4):
        for c in range(3):
            total = None
            for k in range(2):
                x, n = apply0(V1, 1, c, 2 * z + k)
                r = BB[c, 2 * z + k + 2] + n - DD[c, 2 * z + k] * x
                total = r[0:32] if total is None else total + r[0:32]
            RS[c, z] = total

    def row_pairs(ref, c, n):
        return jnp.concatenate(
            [ref[c, z, pl.ds(0, n, 2)] + ref[c, z, pl.ds(1, n, 2)] for z in range(ref.shape[1])], axis=0
        )

    r0, r1, r2 = (row_pairs(RS, c, 16) for c in range(3))
    new = [dot(r0, take_lo) + dot(r1, take_hi), dot(r2, take_lo)]
    for t in range(2):
        value = new[t].reshape(4, 16, 128)
        for z in range(4):
            BB1[t, z + 3, 0:16] = value[z]
            b1_stage[0, t, z] = value[z, 0:4]
            b1_stage[1, t, z] = value[z, 12:16]

    def b1_refs(dt, dh):
        if dt == 0:
            first = 4 if dh > 0 else 3
            return BB1.at[:, pl.ds(first, 3), pl.ds(0, 16)], b1_vert.at[0 if dh > 0 else 1]
        side = 0 if dt < 0 else 1
        if dh == 0:
            return b1_stage.at[side], b1_side.at[side, 0]
        first = 2 if dh > 0 else 0
        return (
            b1_stage.at[side, :, pl.ds(first, 2)],
            b1_side.at[side, 2 if dh > 0 else 1, :, pl.ds(first, 2)],
        )

    b1_moves = near_copies(b1_send, b1_recv, b1_refs)
    start(b1_moves)

    lane1 = iota((24, 128), 1)
    col1 = lane1 % 64
    wait_recv(q1_moves)

    def both(x):
        return jnp.where(iota(x.shape, len(x.shape) - 1) < 64, x, 0.0)

    for z in range(-4, 8):
        if z < 0:
            centre = jnp.where(below, q1_vert[0, z + 4], 0.0)
            lo = jnp.where(jnp.logical_and(below, before), q1_side[1, 2, z + 4], 0.0)
            hi = jnp.where(jnp.logical_and(below, after), q1_side[0, 2, z + 4], 0.0)
        elif z < 4:
            centre = q1[z]
            lo = jnp.where(before, q1_side[1, 1, z], 0.0)
            hi = jnp.where(after, q1_side[0, 1, z], 0.0)
        else:
            centre = jnp.where(above, q1_vert[1, z - 4], 0.0)
            lo = jnp.where(jnp.logical_and(above, before), q1_side[1, 0, z - 4], 0.0)
            hi = jnp.where(jnp.logical_and(above, after), q1_side[0, 0, z - 4], 0.0)
        q = jnp.concatenate([centre, hi, lo], axis=0)
        other = pltpu.roll(q, 64, 1)
        S1[z + 4] = jnp.where(lane1 < 64, q, other)
        if z == 0:
            spring1 = jnp.where(lane1 < 64, other, q)
    for z in range(-4, 7):
        HZ1[z + 4] = S1[z + 4] + S1[z + 5]
    for z in range(-3, 7):
        s = S1[z + 4]
        h_ru = s + pltpu.roll(s, 23, 0)
        h_rl = pltpu.roll(h_ru, 1, 0)
        f_cu = s + jnp.where(col1 < 63, pltpu.roll(s, 127, 1), 0.0)
        f_cl = s + jnp.where(col1 > 0, pltpu.roll(s, 1, 1), 0.0)
        HR1[0, z + 3] = h_rl
        HR1[1, z + 3] = h_ru
        HC1[0, z + 3] = jnp.where(col1 > 0, f_cl, 0.0)
        HC1[1, z + 3] = jnp.where(col1 < 63, f_cu, 0.0)
        f = [HZ1[z + 3] + HZ1[z + 4], h_rl + h_ru, f_cl + f_cu]
        total = f[0] + f[1] + f[2]
        if z == 0:
            total = total + spring1
        for t in range(2):
            d = total + (jnp.where(lane1 < 64, f[0], f[1]) if t == 0 else f[2])
            WH1[t, z + 3] = jnp.where(s > 0.0, OMEGA / jnp.where(s > 0.0, d, 1.0), 0.0)
            if 0 <= z < 4:
                DD1[t, z] = d

    wait_recv(b1_moves)
    for t in range(2):
        for z in range(-3, 7):
            if z < 0:
                BB1[t, z + 3, 0:16] = jnp.where(below, b1_vert[0, t, z + 3], 0.0)
                if z < -2:
                    lo = jnp.zeros((4, 128), F32)
                    hi = lo
                else:
                    lo = jnp.where(jnp.logical_and(below, before), b1_side[1, 2, t, z + 4], 0.0)
                    hi = jnp.where(jnp.logical_and(below, after), b1_side[0, 2, t, z + 4], 0.0)
            elif z < 4:
                lo = jnp.where(before, b1_side[1, 0, t, z], 0.0)
                hi = jnp.where(after, b1_side[0, 0, t, z], 0.0)
            else:
                BB1[t, z + 3, 0:16] = jnp.where(above, b1_vert[1, t, z - 4], 0.0)
                if z > 5:
                    lo = jnp.zeros((4, 128), F32)
                    hi = lo
                else:
                    lo = jnp.where(jnp.logical_and(above, before), b1_side[1, 1, t, z - 4], 0.0)
                    hi = jnp.where(jnp.logical_and(above, after), b1_side[0, 1, t, z - 4], 0.0)
            BB1[t, z + 3, 16:24] = jnp.concatenate([hi, lo], axis=0)

    for z in range(-3, 7):
        for t in range(2):
            VA1[t, z + 3] = WH1[t, z + 3] * BB1[t, z + 3]

    def apply1(v, off, t, z):
        x = v[t, z + off]
        a = HZ1[z + 3] * v[t, z + off - 1] + HZ1[z + 4] * v[t, z + off + 1]
        b = HR1[0, z + 3] * pltpu.roll(x, 1, 0) + HR1[1, z + 3] * pltpu.roll(x, 23, 0)
        e = HC1[0, z + 3] * pltpu.roll(x, 1, 1) + HC1[1, z + 3] * pltpu.roll(x, 127, 1)
        return x, (a + b + e) + (jnp.where(lane1 < 64, a, b) if t == 0 else e)

    for z in range(-2, 6):
        for t in range(2):
            x, n = apply1(VA1, 3, t, z)
            VB1[t, z + 2] = KEEP * x + WH1[t, z + 3] * (BB1[t, z + 3] + n)
    for z in range(2):
        for t in range(2):
            total = None
            for k in range(2):
                x, n = apply1(VB1, 2, t, 2 * z + k)
                r = BB1[t, 2 * z + k + 3] + n - DD1[t, 2 * z + k] * x
                total = r[0:16] if total is None else total + r[0:16]
            RS1[t, z] = total
    down_a = one_hot((128, 128), lambda l, j: l // 2 == j)
    down_b = one_hot((128, 128), lambda l, j: jnp.logical_and(l < 64, l // 2 == j - 64))
    b2_own[...] = (dot(row_pairs(RS1, 0, 8), down_a) + dot(row_pairs(RS1, 1, 8), down_b)).reshape(2, 8, 128)
    b2_moves = far_copies(b2_send, b2_recv, b2_own, b2)
    start(b2_moves)
    b2[pl.ds(2 * h, 2), 16:24] = b2_own[...]

    lane2 = iota((40, 128), 1)
    row2 = iota((40, 128), 0)
    col2 = lane2 % 32
    real = lane2 < 96
    slot = row2 // 8 + (i - 2)
    inside = jnp.logical_and(slot >= 0, slot < tiles)
    keep = jnp.logical_and(inside, real)
    wait_recv(q2_moves)

    def pick(a, b, e):
        return jnp.where(lane2 < 32, a, jnp.where(lane2 < 64, b, e))

    q = jnp.where(inside, q2[0], 0.0)
    spring2 = pick(pltpu.roll(q, 32, 1), pltpu.roll(q, 64, 1), pltpu.roll(q, 96, 1))
    odd_row, odd_col = row2 % 2 == 1, lane2 % 2 == 1

    def pair_sum(x):
        x = x + jnp.where(odd_row, pltpu.roll(x, 1, 0), pltpu.roll(x, 39, 0))
        return x + jnp.where(odd_col, pltpu.roll(x, 1, 1), pltpu.roll(x, 127, 1))

    def faces(s_of, depth, step, spring, hz, hr, hc, wh, dd):
        for z in range(depth - 1):
            hz[z] = s_of(z) + s_of(z + 1)
        for z in range(depth):
            s = s_of(z)
            h_ru = s + pltpu.roll(s, 40 - step, 0)
            h_rl = pltpu.roll(h_ru, step, 0)
            first, last = col2 < step, col2 >= 32 - step
            f_cu = s + jnp.where(last, 0.0, pltpu.roll(s, 128 - step, 1))
            f_cl = s + jnp.where(first, 0.0, pltpu.roll(s, step, 1))
            hr[0, z] = h_rl
            hr[1, z] = h_ru
            hc[0, z] = jnp.where(first, 0.0, f_cl)
            hc[1, z] = jnp.where(last, 0.0, f_cu)
            f_z = (hz[z - 1] if z > 0 else s) + (hz[z] if z < depth - 1 else s)
            f_r, f_c = h_rl + h_ru, f_cl + f_cu
            d = (f_z + f_r + f_c) + pick(f_z, f_r, f_c)
            if z == 0:
                d = d + spring
            wh[z] = jnp.where(s > 0.0, OMEGA / jnp.where(s > 0.0, d, 1.0), 0.0)
            if dd is not None:
                dd[z] = d

    def s2(z):
        return jnp.where(keep, q2[z], 0.0)

    faces(s2, 8, 1, spring2, HZ2, HR2, HC2, WH2, DD2)
    for z in range(4):
        S3[z] = 0.5 * pair_sum(s2(2 * z) + s2(2 * z + 1))
    faces(lambda z: S3[z], 4, 2, pair_sum(spring2), HZ3, HR3, HC3, WH3, None)

    def apply2(v, z, depth, step, hz, hr, hc):
        x = v[z]
        a = None
        if z > 0:
            a = hz[z - 1] * v[z - 1]
        if z < depth - 1:
            up = hz[z] * v[z + 1]
            a = up if a is None else a + up
        b = hr[0, z] * pltpu.roll(x, step, 0) + hr[1, z] * pltpu.roll(x, 40 - step, 0)
        e = hc[0, z] * pltpu.roll(x, step, 1) + hc[1, z] * pltpu.roll(x, 128 - step, 1)
        return x, (a + b + e) + pick(a, b, e)

    wait_recv(b2_moves)
    for z in range(8):
        b = jnp.where(keep, b2[z], 0.0)
        b2[z] = b
        VA2[z] = WH2[z] * b
    for z in range(8):
        x, n = apply2(VA2, z, 8, 1, HZ2, HR2, HC2)
        VB2[z] = KEEP * x + WH2[z] * (b2[z] + n)
    for z in range(4):
        total = None
        for k in range(2):
            x, n = apply2(VB2, 2 * z + k, 8, 1, HZ2, HR2, HC2)
            r = b2[2 * z + k] + n - DD2[2 * z + k] * x
            total = r if total is None else total + r
        total = pair_sum(total)
        BB3[z] = total
        V3[0, z] = WH3[z] * total
    for turn in range(5):
        now, later = turn % 2, (turn + 1) % 2
        for z in range(4):
            x, n = apply2(V3.at[now], z, 4, 2, HZ3, HR3, HC3)
            V3[later, z] = KEEP * x + WH3[z] * (BB3[z] + n)
    for z in range(8):
        VB2[z] = VB2[z] + V3[1, z // 2]
    PO2[0] = jnp.zeros((24, 128), F32)
    PO2[9] = jnp.zeros((24, 128), F32)
    for z in range(8):
        x, n = apply2(VB2, z, 8, 1, HZ2, HR2, HC2)
        PO2[z + 1] = (KEEP * x + WH2[z] * (b2[z] + n))[8:32]

    up_a = one_hot((128, 128), lambda l, j: l == j // 2)
    up_b = one_hot((128, 128), lambda l, j: jnp.logical_and(j < 64, l == 64 + j // 2))
    coarse = PO2[pl.ds(2 * h, 4)].reshape(96, 128)
    for t, m in enumerate((up_a, up_b)):
        e = dot(coarse, m).reshape(4, 24, 128)
        for k in range(4):
            T1[t, k, pl.ds(0, 24, 2)] = e[k]
            T1[t, k, pl.ds(1, 24, 2)] = e[k]
    for z in range(-2, 6):
        for t in range(2):
            k = (z + 2) // 2
            tail = jnp.where(sub8 < 4, T1[t, k, 32:40], T1[t, k, 8:16])
            e = jnp.concatenate([T1[t, k, 16:32], tail], axis=0)
            VB1[t, z + 2] = VB1[t, z + 2] + e
    for z in range(-1, 5):
        for t in range(2):
            x, n = apply1(VB1, 2, t, z)
            PO1[t, z + 1] = KEEP * x + WH1[t, z + 3] * (BB1[t, z + 3] + n)

    up_lo = one_hot((128, 128), lambda l, j: l == j // 2)
    up_hi = one_hot((128, 128), lambda l, j: l == 64 + j // 2)
    for c in range(3):
        e = dot(PO1[c // 2].reshape(144, 128), up_hi if c == 1 else up_lo).reshape(6, 24, 128)
        for k in range(6):
            T0[c, k, pl.ds(0, 24, 2)] = e[k]
            T0[c, k, pl.ds(1, 24, 2)] = e[k]
    for z in range(-1, 9):
        for c in range(3):
            k = (z + 2) // 2
            tail = jnp.where(sub8 < 4, T0[c, k, 32:40], T0[c, k, 40:48])
            V1[c, z + 1] = V1[c, z + 1] + jnp.concatenate([T0[c, k, 0:32], tail], axis=0)
    for z in range(8):
        for c in range(3):
            x, n = apply0(V1, 1, c, z)
            out[c, z] = (KEEP * x + WH[c, z + 2] * (BB[c, z + 2] + n))[0:32]

    for moves in (label_moves, q1_moves, q2_moves, b1_moves, b2_moves):
        wait_send(moves)


def solution(mesh):
    heights, tiles = mesh.shape["height"], mesh.shape["tile"]

    def vmem(*shape, dtype=F32):
        return pltpu.VMEM(shape, dtype)

    i32 = jnp.int32
    scratch = [
        vmem(8, 32, 128, dtype=i32), vmem(2, 32, 128, dtype=i32),
        vmem(3, 32, 128, dtype=i32), vmem(3, 32, 128, dtype=i32),
        vmem(2, 10, 4, 128, dtype=i32), vmem(2, 2, 2, 4, 128, dtype=i32), vmem(2, 10, 4, 128, dtype=i32),
        vmem(4, 16, 128), vmem(2, 4, 16, 128), vmem(2, 3, 4, 4, 128), vmem(2, 4, 4, 128),
        vmem(8, 40, 128), vmem(2, 8, 128),
        vmem(2, 2, 3, 16, 128), vmem(2, 3, 2, 4, 4, 128), vmem(2, 2, 4, 4, 128),
        vmem(8, 40, 128), vmem(2, 8, 128),
        vmem(14, 40, 128), vmem(3, 14, 40, 128), vmem(13, 40, 128), vmem(2, 12, 40, 128), vmem(2, 12, 40, 128),
        vmem(3, 12, 40, 128), vmem(3, 12, 40, 128), vmem(3, 8, 40, 128), vmem(3, 12, 40, 128),
        vmem(3, 10, 40, 128), vmem(3, 4, 32, 128),
        vmem(12, 24, 128), vmem(11, 24, 128), vmem(2, 10, 24, 128), vmem(2, 10, 24, 128), vmem(2, 10, 24, 128),
        vmem(2, 10, 24, 128), vmem(2, 4, 24, 128), vmem(2, 10, 24, 128), vmem(2, 8, 24, 128),
        vmem(2, 2, 16, 128), vmem(2, 6, 24, 128),
        vmem(7, 40, 128), vmem(2, 8, 40, 128), vmem(2, 8, 40, 128), vmem(8, 40, 128), vmem(8, 40, 128),
        vmem(8, 40, 128), vmem(8, 40, 128), vmem(10, 24, 128), vmem(2, 4, 48, 128),
        vmem(4, 40, 128), vmem(3, 40, 128), vmem(2, 4, 40, 128), vmem(2, 4, 40, 128), vmem(4, 40, 128),
        vmem(4, 40, 128), vmem(2, 4, 40, 128),
        vmem(3, 6, 48, 128), vmem(2, 4, 32, 128),
        pltpu.SemaphoreType.DMA((2,)),
    ]
    for count in (8, 8, 19, 8, 19):
        scratch += [pltpu.SemaphoreType.DMA((count,)), pltpu.SemaphoreType.DMA((count,))]

    def local(material, clamped, stiffness_table, eigenstrain):
        return pl.pallas_call(
            functools.partial(kernel, heights, tiles),
            out_shape=jax.ShapeDtypeStruct((3, 8, 32, 128), F32),
            in_specs=[
                pl.BlockSpec(memory_space=pl.ANY),
                pl.BlockSpec(memory_space=pl.ANY),
                pl.BlockSpec(memory_space=pltpu.SMEM),
                pl.BlockSpec(memory_space=pltpu.SMEM),
            ],
            out_specs=pl.BlockSpec(memory_space=pltpu.VMEM),
            scratch_shapes=scratch,
            compiler_params=pltpu.CompilerParams(
                collective_id=0, has_side_effects=True, vmem_limit_bytes=40 * 1024 * 1024
            ),
        )(material, clamped, stiffness_table, eigenstrain)

    in_specs = (P("height", "tile", None), P("height", "tile", None), P(), P())
    out_specs = P(None, "height", "tile", None)
    return jax.shard_map(local, mesh=mesh, in_specs=in_specs, out_specs=out_specs, check_vma=False)
```

time: 422 us -> 31.1 us (0.07)
  starting transfers between devices: 215 us -> 0 us
  waiting for transfers between devices: 85.6 us -> 0 us
  local copies, waits for them, and re-layouts: 61.4 us -> 3.89 us
  other arithmetic: 54.1 us -> 0 us
  Pallas kernels: 0 us -> 27.1 us
    ppermute x76 -> x0, starting transfers between devices: 215 us -> none  [the longest x38 115 us: passed_along(): return lax.ppermute(x, axis, pairs)]
    ppermute x76 -> x0, waiting for transfers between devices: 85.6 us -> none  [the longest x38 81.8 us: passed_along(): return lax.ppermute(x, axis, pairs)]
    reshape x9 -> x0, local copies, waits for them, and re-layouts: 52.3 us -> none  [the longest x5 51.2 us: block_sum(): field.reshape(dims_now[0], dims_now[1] // 2, 2, dims_now[2] // 2, 2, dims...]
    pallas_call x0 -> x1, Pallas kernels: none -> 27.1 us  [local(): pl.pallas_call(functools.partial(kernel, heights, tiles), out_shape=jax.S...]
    add x21 -> x0, other arithmetic: 26.5 us -> none  [the longest x5 10.8 us: coefficients(): low_face + high_face]
    reduce_sum x13 -> x0, other arithmetic: 20.8 us -> none  [block_sum(): return shaped.sum(axis=(2, 4, 6))]
    slice x75 -> x0, local copies, waits for them, and re-layouts: 4.68 us -> none  [the longest x2 2.05 us: lookup(): result = result + (labels == label_id).astype(table.dtype) * table[label_id]]
  transfers between devices with their start and end apart: 76 -> 0, of which waited for: 17 -> 0; matrix products, arithmetic and copies ran while one was open for 10% -> 0% of each run, Pallas kernels for 0% -> 0%
where the time goes in v1:
time: 31.1 us; the launch traced here: 31 us
  Pallas kernels  27.1 us (87%)
  local copies, waits for them, and re-layouts  3.89 us (13%)
    pallas_call x1, Pallas kernels, local(): pl.pallas_call(functools.partial(kernel, heights, tiles), out_shape=jax.S...  27.1 us
    unnamed x9, local copies, waits for them, and re-layouts  3.89 us

profile of v1, /device:TPU:103, one launch (start us, length us, event | category | flops | bytes accessed | tf_op | source)
XLA Modules:
  0.0 31.0 jit_solution(14246834527993776079)
XLA Ops:
  0.0 0.0 copy-start
  0.0 0.9 %copy-done = s32[8,32,128]{2,1,0:T(8,128)S(1)} copy-done((s32[8,32,128]{2,1,0:T(8,128)S(1)}, s32[8,32,128]{2,1,0:T(8,128)}, u32[]{:S(2)}) %copy-start) | copy-done | bytes 131096
  0.9 0.0 copy-start.1
  0.9 0.9 %copy-done.1 = s32[8,32,128]{2,1,0:T(8,128)S(1)} copy-done((s32[8,32,128]{2,1,0:T(8,128)S(1)}, s32[8,32,128]{2,1,0:T(8,128)}, u32[]{:S(2)}) %copy-start.1) | copy-done | bytes 131096
  1.8 0.0 copy-start.2
  1.8 0.7 %copy-done.2 = f32[3,3]{1,0:T(4,128)S(1)} copy-done((f32[3,3]{1,0:T(4,128)S(1)}, f32[3,3]{1,0:T(4,128)}, u32[]{:S(2)}) %copy-start.2) | copy-done | bytes 60
  2.5 0.0 copy-start.3
  2.5 0.7 %copy-done.3 = f32[3]{0:T(128)S(1)} copy-done((f32[3]{0:T(128)S(1)}, f32[3]{0:T(128)}, u32[]{:S(2)}) %copy-start.3) | copy-done | bytes 36
  3.1 27.1 %shard_map.46 = f32[3,8,32,128]{3,2,1,0:T(8,128)S(1)} custom-call(s32[8,32,128]{2,1,0:T(8,128)S(1)} %copy-done, s32[8,32,128]{2,1,0:T(8,128)S(1)} %copy-done.1, f32[3]{0:T(128)S(1)} %copy-done.3, f32[3,3]{1,0:T(4,128)S(1)} %copy-done.2), custom_call_target="tpu_custom_call" | custom-call | tf_op jit(solution)/shard_map/pallas_call | solution.py:591
  30.2 0.7 %copy.6 = f32[3,8,32,128]{3,2,1,0:T(8,128)} copy(f32[3,8,32,128]{3,2,1,0:T(8,128)S(1)} %shard_map.46) | data formatting | bytes 786432
Async XLA Ops:
  0.0 0.9 %copy-start = (s32[8,32,128]{2,1,0:T(8,128)S(1)}, s32[8,32,128]{2,1,0:T(8,128)}, u32[]{:S(2)}) copy-start(s32[8,32,128]{2,1,0:T(8,128)} %mat_hbm.1) | copy-start | bytes 393220
  0.9 0.9 %copy-start.1 = (s32[8,32,128]{2,1,0:T(8,128)S(1)}, s32[8,32,128]{2,1,0:T(8,128)}, u32[]{:S(2)}) copy-start(s32[8,32,128]{2,1,0:T(8,128)} %clamp_hbm.1) | copy-start | bytes 393220
  1.8 0.7 %copy-start.2 = (f32[3,3]{1,0:T(4,128)S(1)}, f32[3,3]{1,0:T(4,128)}, u32[]{:S(2)}) copy-start(f32[3,3]{1,0:T(4,128)} %eigen.1) | copy-start | bytes 112
  2.5 0.7 %copy-start.3 = (f32[3]{0:T(128)S(1)}, f32[3]{0:T(128)}, u32[]{:S(2)}) copy-start(f32[3]{0:T(128)} %table.1) | copy-start | bytes 40

commit v2 on v1

--- a/solution.py
+++ b/solution.py
@@ -12,8 +12,13 @@
 KEEP = 1.0 - OMEGA
 F32 = jnp.float32
 HI = lax.Precision.HIGHEST
-NEAR = tuple((dt, dh) for dt in (-1, 0, 1) for dh in (-1, 0, 1) if (dt, dh) != (0, 0))
-FAR = tuple((dt, k) for dt in (-2, -1, 0, 1, 2) for k in (0, 1, 2, 3) if (dt, k) != (0, 0))
+NEAR = ((-1, -1), (-1, 1), (1, -1), (1, 1), (-1, 0), (1, 0), (0, -1), (0, 1))
+FAR = tuple(
+    sorted(
+        ((dt, k) for dt in (-2, -1, 0, 1, 2) for k in (0, 1, 2, 3) if (dt, k) != (0, 0)),
+        key=lambda move: (-abs(move[0]), -min(move[1], 4 - move[1]), move),
+    )
+)
 
 
 def iota(shape, axis):
@@ -33,9 +38,11 @@
     tiles,
     mat_hbm,
     clamp_hbm,
+    table_hbm,
+    eigen_hbm,
+    out,
     table,
     eigen,
-    out,
     mat,
     cl,
     m_lo, m_hi, m_side, m_corner, m_stage,
@@ -56,8 +63,8 @@
 
     in_mat = pltpu.make_async_copy(mat_hbm, mat, local_sem.at[0])
     in_cl = pltpu.make_async_copy(clamp_hbm.at[pl.ds(0, 2)], cl, local_sem.at[1])
-    in_mat.start()
-    in_cl.start()
+    in_table = pltpu.make_async_copy(table_hbm, table, local_sem.at[2])
+    in_eigen = pltpu.make_async_copy(eigen_hbm, eigen, local_sem.at[3])
 
     def tile_ok(dt):
         return jnp.logical_and(i + dt >= 0, i + dt < tiles)
@@ -68,6 +75,7 @@
     def far_id(dt, k):
         return {"tile": i + dt, "height": lax.rem(h + k, heights)}
 
+    in_mat.start()
     barrier = pltpu.get_barrier_semaphore()
     for dt, k in FAR:
         @pl.when(tile_ok(dt))
@@ -77,6 +85,9 @@
             )
     reach = sum(tile_ok(dt).astype(jnp.int32) for dt in (-2, -1, 0, 1, 2))
 
+    in_cl.start()
+    in_table.start()
+    in_eigen.start()
     in_mat.wait()
     in_cl.wait()
     for z in range(8):
@@ -141,6 +152,9 @@
 
     label_moves = near_copies(m_send, m_recv, label_refs)
     start(label_moves)
+
+    in_table.wait()
+    in_eigen.wait()
 
     st = [table[n] for n in range(3)]
     stress = [[table[n] * eigen[n, c] for c in range(3)] for n in range(3)]
@@ -564,6 +578,7 @@
 
     i32 = jnp.int32
     scratch = [
+        pltpu.SMEM((3,), F32), pltpu.SMEM((3, 3), F32),
         vmem(8, 32, 128, dtype=i32), vmem(2, 32, 128, dtype=i32),
         vmem(3, 32, 128, dtype=i32), vmem(3, 32, 128, dtype=i32),
         vmem(2, 10, 4, 128, dtype=i32), vmem(2, 2, 2, 4, 128, dtype=i32), vmem(2, 10, 4, 128, dtype=i32),
@@ -582,7 +597,7 @@
         vmem(4, 40, 128), vmem(3, 40, 128), vmem(2, 4, 40, 128), vmem(2, 4, 40, 128), vmem(4, 40, 128),
         vmem(4, 40, 128), vmem(2, 4, 40, 128),
         vmem(3, 6, 48, 128), vmem(2, 4, 32, 128),
-        pltpu.SemaphoreType.DMA((2,)),
+        pltpu.SemaphoreType.DMA((4,)),
     ]
     for count in (8, 8, 19, 8, 19):
         scratch += [pltpu.SemaphoreType.DMA((count,)), pltpu.SemaphoreType.DMA((count,))]
@@ -592,17 +607,17 @@
             functools.partial(kernel, heights, tiles),
             out_shape=jax.ShapeDtypeStruct((3, 8, 32, 128), F32),
             in_specs=[
-                pl.BlockSpec(memory_space=pl.ANY),
-                pl.BlockSpec(memory_space=pl.ANY),
-                pl.BlockSpec(memory_space=pltpu.SMEM),
-                pl.BlockSpec(memory_space=pltpu.SMEM),
+                pl.BlockSpec(memory_space=pltpu.HBM),
+                pl.BlockSpec(memory_space=pltpu.HBM),
+                pl.BlockSpec(memory_space=pltpu.HBM),
+                pl.BlockSpec(memory_space=pltpu.HBM),
             ],
             out_specs=pl.BlockSpec(memory_space=pltpu.VMEM),
             scratch_shapes=scratch,
             compiler_params=pltpu.CompilerParams(
                 collective_id=0, has_side_effects=True, vmem_limit_bytes=40 * 1024 * 1024
             ),
-        )(material, clamped, stiffness_table, eigenstrain)
+        )(*(pltpu.with_memory_space_constraint(x, pltpu.HBM) for x in (material, clamped, stiffness_table, eigenstrain)))
 
     in_specs = (P("height", "tile", None), P("height", "tile", None), P(), P())
     out_specs = P(None, "height", "tile", None)

time: 31.1 us -> 26.1 us (0.84)
  local copies, waits for them, and re-layouts: 3.89 us -> 0.75 us
  Pallas kernels: 27.1 us -> 25.2 us
    unnamed x9 -> x1, local copies, waits for them, and re-layouts: 3.89 us -> 0.75 us
    pallas_call x1, Pallas kernels: 27.1 us -> 25.2 us  [local(): pl.pallas_call(functools.partial(kernel, heights, tiles), out_shape=jax.S...]
where the time goes in v2:
time: 26.1 us; the launch traced here: 26 us
  Pallas kernels  25.2 us (97%)
  local copies, waits for them, and re-layouts  0.75 us (3%)
    pallas_call x1, Pallas kernels, local(): pl.pallas_call(functools.partial(kernel, heights, tiles), out_shape=jax.S...  25.2 us
    unnamed x1, local copies, waits for them, and re-layouts  0.75 us

profile of v2, /device:TPU:103, one launch (start us, length us, event | category | flops | bytes accessed | tf_op | source)
XLA Modules:
  0.0 26.0 jit_solution(5163699829540872121)
XLA Ops:
  0.0 25.2 %shard_map.46 = f32[3,8,32,128]{3,2,1,0:T(8,128)S(1)} custom-call(s32[8,32,128]{2,1,0:T(8,128)} %mat_hbm.1, s32[8,32,128]{2,1,0:T(8,128)} %clamp_hbm.1, f32[3]{0:T(128)} %table_hbm.1, f32[3,3]{1,0:T(4,128)} %eigen_hbm.1), custom_call_target="tpu_custom_call" | custom-call | tf_op jit(solution)/shard_map/pallas_call | solution.py:606
  25.2 0.7 %copy.6 = f32[3,8,32,128]{3,2,1,0:T(8,128)} copy(f32[3,8,32,128]{3,2,1,0:T(8,128)S(1)} %shard_map.46) | data formatting | bytes 786432

commit v3 on v2

--- a/solution.py
+++ b/solution.py
@@ -77,13 +77,14 @@
 
     in_mat.start()
     barrier = pltpu.get_barrier_semaphore()
-    for dt, k in FAR:
-        @pl.when(tile_ok(dt))
+    for dt, dh in NEAR:
+        @pl.when(near_ok(dt, dh))
         def _():
             pl.semaphore_signal(
-                barrier, inc=1, device_id=far_id(dt, k), device_id_type=pl.DeviceIdType.MESH
+                barrier, inc=1, device_id={"tile": i + dt, "height": h + dh},
+                device_id_type=pl.DeviceIdType.MESH,
             )
-    reach = sum(tile_ok(dt).astype(jnp.int32) for dt in (-2, -1, 0, 1, 2))
+    reach = sum(near_ok(dt, dh).astype(jnp.int32) for dt, dh in NEAR)
 
     in_cl.start()
     in_table.start()
@@ -97,7 +98,7 @@
         m_stage[0, 8 + z] = cl[z, 0:4]
         m_stage[1, 8 + z] = cl[z, 28:32]
 
-    pl.semaphore_wait(barrier, 4 * reach - 1)
+    pl.semaphore_wait(barrier, reach)
 
     def near_copies(send, recv, refs):
         copies = []
@@ -122,6 +123,27 @@
             )
             copies.append((copy, tile_ok(dt), tile_ok(-dt)))
         return copies
+
+    def ends_apart(dh):
+        if dh == 1:
+            return h == heights - 1
+        if dh == 3:
+            return h == 0
+        return None
+
+    def start_far(copies, apart):
+        for (_, dh), (copy, sends, _) in zip(FAR, copies):
+            wide = ends_apart(dh)
+            if wide is None:
+                if apart:
+                    continue
+                cond = sends
+            else:
+                cond = jnp.logical_and(sends, wide if apart else jnp.logical_not(wide))
+
+            @pl.when(cond)
+            def _():
+                copy.start()
 
     def start(copies):
         for copy, sends, _ in copies:
@@ -205,7 +227,6 @@
     ).astype(F32)
     q2_own[...] = dot(q_rows, down_q).reshape(2, 8, 128)
     q2_moves = far_copies(q2_send, q2_recv, q2_own, q2)
-    start(q2_moves)
     q2[pl.ds(2 * h, 2), 16:24] = q2_own[...]
 
     lane = iota((40, 128), 1)
@@ -335,6 +356,7 @@
 
     b1_moves = near_copies(b1_send, b1_recv, b1_refs)
     start(b1_moves)
+    start_far(q2_moves, False)
 
     lane1 = iota((24, 128), 1)
     col1 = lane1 % 64
@@ -384,6 +406,7 @@
                 DD1[t, z] = d
 
     wait_recv(b1_moves)
+    start_far(q2_moves, True)
     for t in range(2):
         for z in range(-3, 7):
             if z < 0:

time: 26.1 us -> 25 us (0.958)
  Pallas kernels: 25.2 us -> 24 us
    pallas_call x1, Pallas kernels: 25.2 us -> 24 us  [local(): pl.pallas_call(functools.partial(kernel, heights, tiles), out_shape=jax.S...]
where the time goes in v3:
time: 25 us; the launch traced here: 24.7 us
  Pallas kernels  24 us (96%)
  local copies, waits for them, and re-layouts  0.75 us (3%)
    pallas_call x1, Pallas kernels, local(): pl.pallas_call(functools.partial(kernel, heights, tiles), out_shape=jax.S...  24 us
    unnamed x1, local copies, waits for them, and re-layouts  0.75 us

profile of v3, /device:TPU:103, one launch (start us, length us, event | category | flops | bytes accessed | tf_op | source)
XLA Modules:
  0.0 24.7 jit_solution(17701177281371490073)
XLA Ops:
  0.0 24.0 %shard_map.46 = f32[3,8,32,128]{3,2,1,0:T(8,128)S(1)} custom-call(s32[8,32,128]{2,1,0:T(8,128)} %mat_hbm.1, s32[8,32,128]{2,1,0:T(8,128)} %clamp_hbm.1, f32[3]{0:T(128)} %table_hbm.1, f32[3,3]{1,0:T(4,128)} %eigen_hbm.1), custom_call_target="tpu_custom_call" | custom-call | tf_op jit(solution)/shard_map/pallas_call | solution.py:629
  24.0 0.7 %copy.6 = f32[3,8,32,128]{3,2,1,0:T(8,128)} copy(f32[3,8,32,128]{3,2,1,0:T(8,128)S(1)} %shard_map.46) | data formatting | bytes 786432

commit v4 on v3

--- a/solution.py
+++ b/solution.py
@@ -13,6 +13,7 @@
 F32 = jnp.float32
 HI = lax.Precision.HIGHEST
 NEAR = ((-1, -1), (-1, 1), (1, -1), (1, 1), (-1, 0), (1, 0), (0, -1), (0, 1))
+UPDOWN = ((0, -1), (0, 1))
 FAR = tuple(
     sorted(
         ((dt, k) for dt in (-2, -1, 0, 1, 2) for k in (0, 1, 2, 3) if (dt, k) != (0, 0)),
@@ -48,9 +49,9 @@
     m_lo, m_hi, m_side, m_corner, m_stage,
     q1, q1_vert, q1_side, q1_stage,
     q2, q2_own,
-    b1_vert, b1_side, b1_stage,
+    b1_vert,
     b2, b2_own,
-    S, SG, HZ, HR, HC, BB, WH, DD, V0, V1, RS,
+    S, SG, HZ, HR, HC, BB, WH, DD, V0, V1, RS, EX,
     S1, HZ1, HR1, HC1, BB1, WH1, DD1, VA1, VB1, RS1, PO1,
     HZ2, HR2, HC2, WH2, DD2, VA2, VB2, PO2, T1,
     S3, HZ3, HR3, HC3, WH3, BB3, V3,
@@ -91,18 +92,18 @@
     in_eigen.start()
     in_mat.wait()
     in_cl.wait()
-    for z in range(8):
-        m_stage[0, z] = mat[z, 0:4]
-        m_stage[1, z] = mat[z, 28:32]
-    for z in range(2):
-        m_stage[0, 8 + z] = cl[z, 0:4]
-        m_stage[1, 8 + z] = cl[z, 28:32]
+    for side, first, edge in ((0, 0, 8), (1, 24, 23)):
+        for z in range(8):
+            m_stage[side, z] = mat[z, first : first + 8]
+        for z in range(2):
+            m_stage[side, 8 + z] = cl[z, first : first + 8]
+        m_stage[side, 10] = mat[:, edge]
 
     pl.semaphore_wait(barrier, reach)
 
-    def near_copies(send, recv, refs):
+    def near_copies(send, recv, refs, moves=NEAR):
         copies = []
-        for k, (dt, dh) in enumerate(NEAR):
+        for k, (dt, dh) in enumerate(moves):
             src, dst = refs(dt, dh)
             copy = pltpu.make_async_remote_copy(
                 src_ref=src, dst_ref=dst, send_sem=send.at[k], recv_sem=recv.at[k],
@@ -169,8 +170,8 @@
         side = 0 if dt < 0 else 1
         if dh == 0:
             return m_stage.at[side], m_side.at[side]
-        first = 6 if dh > 0 else 0
-        return m_stage.at[side, pl.ds(first, 2)], m_corner.at[side, 0 if dh < 0 else 1]
+        first = 5 if dh > 0 else 0
+        return m_stage.at[side, pl.ds(first, 3)], m_corner.at[side, 0 if dh < 0 else 1]
 
     label_moves = near_copies(m_send, m_recv, label_refs)
     start(label_moves)
@@ -229,57 +230,56 @@
     q2_moves = far_copies(q2_send, q2_recv, q2_own, q2)
     q2[pl.ds(2 * h, 2), 16:24] = q2_own[...]
 
-    lane = iota((40, 128), 1)
+    lane = iota((48, 128), 1)
+    row = iota((48, 128), 0)
     sub8 = iota((8, 128), 0)
     wait_recv(label_moves)
     below, above = h > 0, h < heights - 1
     before, after = i > 0, i < tiles - 1
 
-    def side_rows(z, ref_of):
-        lo_ok, lo = ref_of(1)
-        hi_ok, hi = ref_of(0)
-        return jnp.concatenate([jnp.where(hi_ok, hi, -1), jnp.where(lo_ok, lo, -1)], axis=0)
-
     def labels(z):
-        if z < 0:
-            centre = jnp.where(below, m_lo[z + 3], -1)
-            if z < -2:
-                return jnp.concatenate([centre, jnp.full((8, 128), -1, jnp.int32)], axis=0)
-            sides = side_rows(
-                z, lambda s: (jnp.logical_and(below, before if s else after), m_corner[s, 1, z + 2])
-            )
-        elif z < 8:
-            centre = mat[z]
-            sides = side_rows(z, lambda s: (before if s else after, m_side[s, z]))
+        if 0 <= z < 8:
+            centre, hi, lo = mat[z], m_side[0, z], m_side[1, z]
+            centre_ok, hi_ok, lo_ok = None, after, before
         else:
-            centre = jnp.where(above, m_hi[z - 8], -1)
-            if z > 9:
-                return jnp.concatenate([centre, jnp.full((8, 128), -1, jnp.int32)], axis=0)
-            sides = side_rows(
-                z, lambda s: (jnp.logical_and(above, before if s else after), m_corner[s, 0, z - 8])
-            )
-        return jnp.concatenate([centre, sides], axis=0)
+            centre_ok = below if z < 0 else above
+            k = z + 3 if z < 0 else z - 8
+            end = 1 if z < 0 else 0
+            centre = (m_lo if z < 0 else m_hi)[k]
+            hi, lo = m_corner[0, end, k], m_corner[1, end, k]
+            hi_ok, lo_ok = jnp.logical_and(centre_ok, after), jnp.logical_and(centre_ok, before)
+            centre = jnp.where(centre_ok, centre, -1)
+        return jnp.concatenate([centre, jnp.where(hi_ok, hi, -1), jnp.where(lo_ok, lo, -1)], axis=0)
 
     for z in range(-3, 11):
         m = labels(z)
         S[z + 3] = look(m, st)
         for c in range(3):
             SG[c, z + 3] = look(m, [stress[n][c] for n in range(3)])
+    for side, ok in ((0, after), (1, before)):
+        m = jnp.where(ok, m_side[side, 10], -1)
+        EX[side, 0] = look(m, st)
+        EX[side, 1] = look(m, [stress[n][1] for n in range(3)])
     for z in range(-3, 10):
         HZ[z + 3] = S[z + 3] + S[z + 4]
 
     def spring0(z):
         sides = jnp.concatenate(
-            [jnp.where(after, m_side[0, 8 + z], 0), jnp.where(before, m_side[1, 8 + z], 0)], axis=0
+            [jnp.where(after, m_side[0, 8 + z], 0), jnp.where(before, m_side[1, 8 + z], 0)],
+            axis=0,
         )
         return (2.0 * PENALTY * lowest) * jnp.concatenate([cl[z], sides], axis=0).astype(F32)
 
     for z in range(-2, 10):
         s = S[z + 3]
-        s_r = pltpu.roll(s, 39, 0)
+        s_r = pltpu.roll(s, 47, 0)
+        if 0 <= z < 8:
+            s_r = jnp.where(row == 39, EX[0, 0, z : z + 1], s_r)
         s_c = jnp.where(lane < 127, pltpu.roll(s, 127, 1), 0.0)
         h_ru = s + s_r
         h_rl = pltpu.roll(h_ru, 1, 0)
+        if 0 <= z < 8:
+            h_rl = jnp.where(row == 40, s + EX[1, 0, z : z + 1], h_rl)
         f_cu = s + s_c
         f_cl = s + jnp.where(lane > 0, pltpu.roll(s, 1, 1), 0.0)
         HR[0, z + 2] = h_rl
@@ -292,7 +292,11 @@
             total = total + spring0(z)
         g0 = SG[0, z + 2] - SG[0, z + 4]
         x = SG[1, z + 3]
-        g1 = pltpu.roll(x, 1, 0) - pltpu.roll(x, 39, 0)
+        x_l, x_u = pltpu.roll(x, 1, 0), pltpu.roll(x, 47, 0)
+        if 0 <= z < 8:
+            x_l = jnp.where(row == 40, EX[1, 1, z : z + 1], x_l)
+            x_u = jnp.where(row == 39, EX[0, 1, z : z + 1], x_u)
+        g1 = x_l - x_u
         x = SG[2, z + 3]
         g2 = jnp.where(lane > 0, pltpu.roll(x, 1, 1), 0.0) - jnp.where(
             lane < 127, pltpu.roll(x, 127, 1), 0.0
@@ -309,7 +313,7 @@
     def apply0(v, off, c, z):
         x = v[c, z + off]
         a = HZ[z + 2] * v[c, z + off - 1] + HZ[z + 3] * v[c, z + off + 1]
-        b = HR[0, z + 2] * pltpu.roll(x, 1, 0) + HR[1, z + 2] * pltpu.roll(x, 39, 0)
+        b = HR[0, z + 2] * pltpu.roll(x, 1, 0) + HR[1, z + 2] * pltpu.roll(x, 47, 0)
         e = HC[0, z + 2] * pltpu.roll(x, 1, 1) + HC[1, z + 2] * pltpu.roll(x, 127, 1)
         return x, (a + b + e) + (a, b, e)[c]
 
@@ -324,7 +328,7 @@
             for k in range(2):
                 x, n = apply0(V1, 1, c, 2 * z + k)
                 r = BB[c, 2 * z + k + 2] + n - DD[c, 2 * z + k] * x
-                total = r[0:32] if total is None else total + r[0:32]
+                total = r if total is None else total + r
             RS[c, z] = total
 
     def row_pairs(ref, c, n):
@@ -332,29 +336,18 @@
             [ref[c, z, pl.ds(0, n, 2)] + ref[c, z, pl.ds(1, n, 2)] for z in range(ref.shape[1])], axis=0
         )
 
-    r0, r1, r2 = (row_pairs(RS, c, 16) for c in range(3))
+    r0, r1, r2 = (row_pairs(RS, c, 24) for c in range(3))
     new = [dot(r0, take_lo) + dot(r1, take_hi), dot(r2, take_lo)]
     for t in range(2):
-        value = new[t].reshape(4, 16, 128)
+        value = new[t].reshape(4, 24, 128)
         for z in range(4):
-            BB1[t, z + 3, 0:16] = value[z]
-            b1_stage[0, t, z] = value[z, 0:4]
-            b1_stage[1, t, z] = value[z, 12:16]
+            BB1[t, z + 3] = value[z]
 
     def b1_refs(dt, dh):
-        if dt == 0:
-            first = 4 if dh > 0 else 3
-            return BB1.at[:, pl.ds(first, 3), pl.ds(0, 16)], b1_vert.at[0 if dh > 0 else 1]
-        side = 0 if dt < 0 else 1
-        if dh == 0:
-            return b1_stage.at[side], b1_side.at[side, 0]
-        first = 2 if dh > 0 else 0
-        return (
-            b1_stage.at[side, :, pl.ds(first, 2)],
-            b1_side.at[side, 2 if dh > 0 else 1, :, pl.ds(first, 2)],
-        )
-
-    b1_moves = near_copies(b1_send, b1_recv, b1_refs)
+        first = 4 if dh > 0 else 3
+        return BB1.at[:, pl.ds(first, 3)], b1_vert.at[0 if dh > 0 else 1]
+
+    b1_moves = near_copies(b1_send, b1_recv, b1_refs, UPDOWN)
     start(b1_moves)
     start_far(q2_moves, False)
 
@@ -408,27 +401,9 @@
     wait_recv(b1_moves)
     start_far(q2_moves, True)
     for t in range(2):
-        for z in range(-3, 7):
-            if z < 0:
-                BB1[t, z + 3, 0:16] = jnp.where(below, b1_vert[0, t, z + 3], 0.0)
-                if z < -2:
-                    lo = jnp.zeros((4, 128), F32)
-                    hi = lo
-                else:
-                    lo = jnp.where(jnp.logical_and(below, before), b1_side[1, 2, t, z + 4], 0.0)
-                    hi = jnp.where(jnp.logical_and(below, after), b1_side[0, 2, t, z + 4], 0.0)
-            elif z < 4:
-                lo = jnp.where(before, b1_side[1, 0, t, z], 0.0)
-                hi = jnp.where(after, b1_side[0, 0, t, z], 0.0)
-            else:
-                BB1[t, z + 3, 0:16] = jnp.where(above, b1_vert[1, t, z - 4], 0.0)
-                if z > 5:
-                    lo = jnp.zeros((4, 128), F32)
-                    hi = lo
-                else:
-                    lo = jnp.where(jnp.logical_and(above, before), b1_side[1, 1, t, z - 4], 0.0)
-                    hi = jnp.where(jnp.logical_and(above, after), b1_side[0, 1, t, z - 4], 0.0)
-            BB1[t, z + 3, 16:24] = jnp.concatenate([hi, lo], axis=0)
+        for z in range(3):
+            BB1[t, z] = jnp.where(below, b1_vert[0, t, z], 0.0)
+            BB1[t, z + 7] = jnp.where(above, b1_vert[1, t, z], 0.0)
 
     for z in range(-3, 7):
         for t in range(2):
@@ -582,8 +557,7 @@
     for z in range(-1, 9):
         for c in range(3):
             k = (z + 2) // 2
-            tail = jnp.where(sub8 < 4, T0[c, k, 32:40], T0[c, k, 40:48])
-            V1[c, z + 1] = V1[c, z + 1] + jnp.concatenate([T0[c, k, 0:32], tail], axis=0)
+            V1[c, z + 1] = V1[c, z + 1] + T0[c, k]
     for z in range(8):
         for c in range(3):
             x, n = apply0(V1, 1, c, z)
@@ -604,14 +578,14 @@
         pltpu.SMEM((3,), F32), pltpu.SMEM((3, 3), F32),
         vmem(8, 32, 128, dtype=i32), vmem(2, 32, 128, dtype=i32),
         vmem(3, 32, 128, dtype=i32), vmem(3, 32, 128, dtype=i32),
-        vmem(2, 10, 4, 128, dtype=i32), vmem(2, 2, 2, 4, 128, dtype=i32), vmem(2, 10, 4, 128, dtype=i32),
+        vmem(2, 11, 8, 128, dtype=i32), vmem(2, 2, 3, 8, 128, dtype=i32), vmem(2, 11, 8, 128, dtype=i32),
         vmem(4, 16, 128), vmem(2, 4, 16, 128), vmem(2, 3, 4, 4, 128), vmem(2, 4, 4, 128),
         vmem(8, 40, 128), vmem(2, 8, 128),
-        vmem(2, 2, 3, 16, 128), vmem(2, 3, 2, 4, 4, 128), vmem(2, 2, 4, 4, 128),
+        vmem(2, 2, 3, 24, 128),
         vmem(8, 40, 128), vmem(2, 8, 128),
-        vmem(14, 40, 128), vmem(3, 14, 40, 128), vmem(13, 40, 128), vmem(2, 12, 40, 128), vmem(2, 12, 40, 128),
-        vmem(3, 12, 40, 128), vmem(3, 12, 40, 128), vmem(3, 8, 40, 128), vmem(3, 12, 40, 128),
-        vmem(3, 10, 40, 128), vmem(3, 4, 32, 128),
+        vmem(14, 48, 128), vmem(3, 14, 48, 128), vmem(13, 48, 128), vmem(2, 12, 48, 128), vmem(2, 12, 48, 128),
+        vmem(3, 12, 48, 128), vmem(3, 12, 48, 128), vmem(3, 8, 48, 128), vmem(3, 12, 48, 128),
+        vmem(3, 10, 48, 128), vmem(3, 4, 48, 128), vmem(2, 2, 8, 128),
         vmem(12, 24, 128), vmem(11, 24, 128), vmem(2, 10, 24, 128), vmem(2, 10, 24, 128), vmem(2, 10, 24, 128),
         vmem(2, 10, 24, 128), vmem(2, 4, 24, 128), vmem(2, 10, 24, 128), vmem(2, 8, 24, 128),
         vmem(2, 2, 16, 128), vmem(2, 6, 24, 128),
@@ -622,7 +596,7 @@
         vmem(3, 6, 48, 128), vmem(2, 4, 32, 128),
         pltpu.SemaphoreType.DMA((4,)),
     ]
-    for count in (8, 8, 19, 8, 19):
+    for count in (8, 8, 19, 2, 19):
         scratch += [pltpu.SemaphoreType.DMA((count,)), pltpu.SemaphoreType.DMA((count,))]
 
     def local(material, clamped, stiffness_table, eigenstrain):

time: 25 us -> 25.6 us (1.024)
  Pallas kernels: 24 us -> 24.8 us
    pallas_call x1, Pallas kernels: 24 us -> 24.8 us  [local(): pl.pallas_call(functools.partial(kernel, heights, tiles), out_shape=jax.S...]
where the time goes in v4:
time: 25.6 us; the launch traced here: 25.5 us
  Pallas kernels  24.8 us (97%)
  local copies, waits for them, and re-layouts  0.75 us (3%)
    pallas_call x1, Pallas kernels, local(): pl.pallas_call(functools.partial(kernel, heights, tiles), out_shape=jax.S...  24.8 us
    unnamed x1, local copies, waits for them, and re-layouts  0.75 us

profile of v4, /device:TPU:103, one launch (start us, length us, event | category | flops | bytes accessed | tf_op | source)
XLA Modules:
  0.0 25.5 jit_solution(766906380834102388)
XLA Ops:
  0.0 24.8 %shard_map.46 = f32[3,8,32,128]{3,2,1,0:T(8,128)S(1)} custom-call(s32[8,32,128]{2,1,0:T(8,128)} %mat_hbm.1, s32[8,32,128]{2,1,0:T(8,128)} %clamp_hbm.1, f32[3]{0:T(128)} %table_hbm.1, f32[3,3]{1,0:T(4,128)} %eigen_hbm.1), custom_call_target="tpu_custom_call" | custom-call | tf_op jit(solution)/shard_map/pallas_call | solution.py:603
  24.8 0.7 %copy.6 = f32[3,8,32,128]{3,2,1,0:T(8,128)} copy(f32[3,8,32,128]{3,2,1,0:T(8,128)S(1)} %shard_map.46) | data formatting | bytes 786432

commit v5 on v4

--- a/solution.py
+++ b/solution.py
@@ -11,9 +11,10 @@
 OMEGA = 0.6
 KEEP = 1.0 - OMEGA
 F32 = jnp.float32
-HI = lax.Precision.HIGHEST
+BF16 = jnp.bfloat16
 NEAR = ((-1, -1), (-1, 1), (1, -1), (1, 1), (-1, 0), (1, 0), (0, -1), (0, 1))
 UPDOWN = ((0, -1), (0, 1))
+DEEP = tuple(move for move in NEAR if move[1] != 0)
 FAR = tuple(
     sorted(
         ((dt, k) for dt in (-2, -1, 0, 1, 2) for k in (0, 1, 2, 3) if (dt, k) != (0, 0)),
@@ -27,11 +28,16 @@
 
 
 def one_hot(shape, cond):
-    return jnp.where(cond(iota(shape, 0), iota(shape, 1)), 1.0, 0.0).astype(F32)
+    return jnp.where(cond(iota(shape, 0), iota(shape, 1)), 1.0, 0.0).astype(BF16)
 
 
 def dot(a, b):
-    return jnp.dot(a, b, preferred_element_type=F32, precision=HI)
+    hi = a.astype(BF16)
+    rest = a - hi.astype(F32)
+    mid = rest.astype(BF16)
+    lo = (rest - mid.astype(F32)).astype(BF16)
+    parts = (jnp.dot(x, b, preferred_element_type=F32) for x in (lo, mid, hi))
+    return sum(parts)
 
 
 def kernel(
@@ -57,7 +63,7 @@
     S3, HZ3, HR3, HC3, WH3, BB3, V3,
     T0, R4,
     local_sem,
-    m_send, m_recv, q1_send, q1_recv, q2_send, q2_recv, b1_send, b1_recv, b2_send, b2_recv,
+    m_send, m_recv, d_send, d_recv, q1_send, q1_recv, q2_send, q2_recv, b1_send, b1_recv, b2_send, b2_recv,
 ):
     i = lax.axis_index("tile")
     h = lax.axis_index("height")
@@ -78,14 +84,14 @@
 
     in_mat.start()
     barrier = pltpu.get_barrier_semaphore()
-    for dt, dh in NEAR:
-        @pl.when(near_ok(dt, dh))
+    ring = [(dt, k) for dt in (-1, 1, 0) for k in (1, 3, 0) if (dt, k) != (0, 0)]
+    for dt, k in ring:
+        @pl.when(tile_ok(dt))
         def _():
             pl.semaphore_signal(
-                barrier, inc=1, device_id={"tile": i + dt, "height": h + dh},
-                device_id_type=pl.DeviceIdType.MESH,
+                barrier, inc=1, device_id=far_id(dt, k), device_id_type=pl.DeviceIdType.MESH
             )
-    reach = sum(near_ok(dt, dh).astype(jnp.int32) for dt, dh in NEAR)
+    reach = 3 * (tile_ok(-1).astype(jnp.int32) + tile_ok(1).astype(jnp.int32)) + 2
 
     in_cl.start()
     in_table.start()
@@ -125,27 +131,6 @@
             copies.append((copy, tile_ok(dt), tile_ok(-dt)))
         return copies
 
-    def ends_apart(dh):
-        if dh == 1:
-            return h == heights - 1
-        if dh == 3:
-            return h == 0
-        return None
-
-    def start_far(copies, apart):
-        for (_, dh), (copy, sends, _) in zip(FAR, copies):
-            wide = ends_apart(dh)
-            if wide is None:
-                if apart:
-                    continue
-                cond = sends
-            else:
-                cond = jnp.logical_and(sends, wide if apart else jnp.logical_not(wide))
-
-            @pl.when(cond)
-            def _():
-                copy.start()
-
     def start(copies):
         for copy, sends, _ in copies:
             @pl.when(sends)
@@ -166,16 +151,30 @@
 
     def label_refs(dt, dh):
         if dt == 0:
-            return (mat.at[pl.ds(5, 3)], m_lo) if dh > 0 else (mat.at[pl.ds(0, 3)], m_hi)
+            if dh > 0:
+                return mat.at[pl.ds(5, 3)], m_lo.at[pl.ds(4, 3)]
+            return mat.at[pl.ds(0, 3)], m_hi.at[pl.ds(0, 3)]
         side = 0 if dt < 0 else 1
         if dh == 0:
             return m_stage.at[side], m_side.at[side]
-        first = 5 if dh > 0 else 0
-        return m_stage.at[side, pl.ds(first, 3)], m_corner.at[side, 0 if dh < 0 else 1]
+        if dh > 0:
+            return m_stage.at[side, pl.ds(5, 3)], m_corner.at[side, 1, pl.ds(4, 3)]
+        return m_stage.at[side, pl.ds(0, 3)], m_corner.at[side, 0, pl.ds(0, 3)]
+
+    def deep_refs(dt, dh):
+        if dt == 0:
+            if dh > 0:
+                return mat.at[pl.ds(1, 4)], m_lo.at[pl.ds(0, 4)]
+            return mat.at[pl.ds(3, 4)], m_hi.at[pl.ds(3, 4)]
+        side = 0 if dt < 0 else 1
+        if dh > 0:
+            return m_stage.at[side, pl.ds(1, 4)], m_corner.at[side, 1, pl.ds(0, 4)]
+        return m_stage.at[side, pl.ds(3, 4)], m_corner.at[side, 0, pl.ds(3, 4)]
 
     label_moves = near_copies(m_send, m_recv, label_refs)
     start(label_moves)
-
+    deep_moves = near_copies(d_send, d_recv, deep_refs, DEEP)
+    start(deep_moves)
     in_table.wait()
     in_eigen.wait()
 
@@ -225,7 +224,7 @@
     down_q = jnp.where(
         jnp.logical_and(j < 96, jnp.logical_and(l < 64, l // 2 == j % 32)), 0.5,
         jnp.where(jnp.logical_and(j >= 96, l // 2 == j - 64), 1.0, 0.0),
-    ).astype(F32)
+    ).astype(BF16)
     q2_own[...] = dot(q_rows, down_q).reshape(2, 8, 128)
     q2_moves = far_copies(q2_send, q2_recv, q2_own, q2)
     q2[pl.ds(2 * h, 2), 16:24] = q2_own[...]
@@ -234,6 +233,7 @@
     row = iota((48, 128), 0)
     sub8 = iota((8, 128), 0)
     wait_recv(label_moves)
+    start(q2_moves)
     below, above = h > 0, h < heights - 1
     before, after = i > 0, i < tiles - 1
 
@@ -243,25 +243,30 @@
             centre_ok, hi_ok, lo_ok = None, after, before
         else:
             centre_ok = below if z < 0 else above
-            k = z + 3 if z < 0 else z - 8
             end = 1 if z < 0 else 0
-            centre = (m_lo if z < 0 else m_hi)[k]
+            k = z + 7 if z < 0 else z - 8
+            centre = jnp.where(centre_ok, (m_lo if z < 0 else m_hi)[k], -1)
             hi, lo = m_corner[0, end, k], m_corner[1, end, k]
             hi_ok, lo_ok = jnp.logical_and(centre_ok, after), jnp.logical_and(centre_ok, before)
-            centre = jnp.where(centre_ok, centre, -1)
         return jnp.concatenate([centre, jnp.where(hi_ok, hi, -1), jnp.where(lo_ok, lo, -1)], axis=0)
 
-    for z in range(-3, 11):
-        m = labels(z)
-        S[z + 3] = look(m, st)
-        for c in range(3):
-            SG[c, z + 3] = look(m, [stress[n][c] for n in range(3)])
+    def build(zs):
+        for z in zs:
+            m = labels(z)
+            S[z + 7] = look(m, st)
+            for c in range(3):
+                SG[c, z + 7] = look(m, [stress[n][c] for n in range(3)])
+
+    build(range(-3, 11))
     for side, ok in ((0, after), (1, before)):
         m = jnp.where(ok, m_side[side, 10], -1)
         EX[side, 0] = look(m, st)
         EX[side, 1] = look(m, [stress[n][1] for n in range(3)])
-    for z in range(-3, 10):
-        HZ[z + 3] = S[z + 3] + S[z + 4]
+    def between(zs):
+        for z in zs:
+            HZ[z + 7] = S[z + 7] + S[z + 8]
+
+    between(range(-3, 10))
 
     def spring0(z):
         sides = jnp.concatenate(
@@ -270,8 +275,8 @@
         )
         return (2.0 * PENALTY * lowest) * jnp.concatenate([cl[z], sides], axis=0).astype(F32)
 
-    for z in range(-2, 10):
-        s = S[z + 3]
+    def first_sweep(z):
+        s = S[z + 7]
         s_r = pltpu.roll(s, 47, 0)
         if 0 <= z < 8:
             s_r = jnp.where(row == 39, EX[0, 0, z : z + 1], s_r)
@@ -282,74 +287,81 @@
             h_rl = jnp.where(row == 40, s + EX[1, 0, z : z + 1], h_rl)
         f_cu = s + s_c
         f_cl = s + jnp.where(lane > 0, pltpu.roll(s, 1, 1), 0.0)
-        HR[0, z + 2] = h_rl
-        HR[1, z + 2] = h_ru
-        HC[0, z + 2] = jnp.where(lane > 0, f_cl, 0.0)
-        HC[1, z + 2] = jnp.where(lane < 127, f_cu, 0.0)
-        f = [HZ[z + 2] + HZ[z + 3], h_rl + h_ru, f_cl + f_cu]
+        HR[0, z + 6] = h_rl
+        HR[1, z + 6] = h_ru
+        HC[0, z + 6] = jnp.where(lane > 0, f_cl, 0.0)
+        HC[1, z + 6] = jnp.where(lane < 127, f_cu, 0.0)
+        f = [HZ[z + 6] + HZ[z + 7], h_rl + h_ru, f_cl + f_cu]
         total = f[0] + f[1] + f[2]
         if 0 <= z < 2:
             total = total + spring0(z)
-        g0 = SG[0, z + 2] - SG[0, z + 4]
-        x = SG[1, z + 3]
+        g0 = SG[0, z + 6] - SG[0, z + 8]
+        x = SG[1, z + 7]
         x_l, x_u = pltpu.roll(x, 1, 0), pltpu.roll(x, 47, 0)
         if 0 <= z < 8:
             x_l = jnp.where(row == 40, EX[1, 1, z : z + 1], x_l)
             x_u = jnp.where(row == 39, EX[0, 1, z : z + 1], x_u)
         g1 = x_l - x_u
-        x = SG[2, z + 3]
+        x = SG[2, z + 7]
         g2 = jnp.where(lane > 0, pltpu.roll(x, 1, 1), 0.0) - jnp.where(
             lane < 127, pltpu.roll(x, 127, 1), 0.0
         )
         for c, g in enumerate((g0, g1, g2)):
             d = total + f[c]
             w = jnp.where(s > 0.0, OMEGA / jnp.where(s > 0.0, d, 1.0), 0.0)
-            BB[c, z + 2] = g
-            WH[c, z + 2] = w
-            if 0 <= z < 8:
-                DD[c, z] = d
-            V0[c, z + 2] = w * g
+            BB[c, z + 6] = g
+            WH[c, z + 6] = w
+            if -4 <= z < 12:
+                DD[c, z + 4] = d
+            V0[c, z + 6] = w * g
+
+    for z in range(-2, 10):
+        first_sweep(z)
 
     def apply0(v, off, c, z):
         x = v[c, z + off]
-        a = HZ[z + 2] * v[c, z + off - 1] + HZ[z + 3] * v[c, z + off + 1]
-        b = HR[0, z + 2] * pltpu.roll(x, 1, 0) + HR[1, z + 2] * pltpu.roll(x, 47, 0)
-        e = HC[0, z + 2] * pltpu.roll(x, 1, 1) + HC[1, z + 2] * pltpu.roll(x, 127, 1)
+        a = HZ[z + 6] * v[c, z + off - 1] + HZ[z + 7] * v[c, z + off + 1]
+        b = HR[0, z + 6] * pltpu.roll(x, 1, 0) + HR[1, z + 6] * pltpu.roll(x, 47, 0)
+        e = HC[0, z + 6] * pltpu.roll(x, 1, 1) + HC[1, z + 6] * pltpu.roll(x, 127, 1)
         return x, (a + b + e) + (a, b, e)[c]
 
-    for z in range(-1, 9):
-        for c in range(3):
-            x, n = apply0(V0, 2, c, z)
-            V1[c, z + 1] = KEEP * x + WH[c, z + 2] * (BB[c, z + 2] + n)
-
-    for z in range(4):
-        for c in range(3):
-            total = None
-            for k in range(2):
-                x, n = apply0(V1, 1, c, 2 * z + k)
-                r = BB[c, 2 * z + k + 2] + n - DD[c, 2 * z + k] * x
-                total = r if total is None else total + r
-            RS[c, z] = total
-
-    def row_pairs(ref, c, n):
-        return jnp.concatenate(
-            [ref[c, z, pl.ds(0, n, 2)] + ref[c, z, pl.ds(1, n, 2)] for z in range(ref.shape[1])], axis=0
-        )
-
-    r0, r1, r2 = (row_pairs(RS, c, 24) for c in range(3))
-    new = [dot(r0, take_lo) + dot(r1, take_hi), dot(r2, take_lo)]
-    for t in range(2):
-        value = new[t].reshape(4, 24, 128)
-        for z in range(4):
-            BB1[t, z + 3] = value[z]
+    def second_sweep(zs):
+        for z in zs:
+            for c in range(3):
+                x, n = apply0(V0, 6, c, z)
+                V1[c, z + 5] = KEEP * x + WH[c, z + 6] * (BB[c, z + 6] + n)
+
+    def pairs(ref, c, z, n):
+        return ref[c, z, pl.ds(0, n, 2)] + ref[c, z, pl.ds(1, n, 2)]
+
+    def restrict(zs):
+        for z in zs:
+            for c in range(3):
+                total = None
+                for k in range(2):
+                    x, n = apply0(V1, 5, c, 2 * z + k)
+                    r = BB[c, 2 * z + k + 6] + n - DD[c, 2 * z + k + 4] * x
+                    total = r if total is None else total + r
+                RS[c, z + 2] = total
+            BB1[0, z + 3] = dot(pairs(RS, 0, z + 2, 24), take_lo) + dot(pairs(RS, 1, z + 2, 24), take_hi)
+            BB1[1, z + 3] = dot(pairs(RS, 2, z + 2, 24), take_lo)
+
+    second_sweep(range(-1, 9))
+    restrict(range(0, 4))
 
     def b1_refs(dt, dh):
-        first = 4 if dh > 0 else 3
-        return BB1.at[:, pl.ds(first, 3)], b1_vert.at[0 if dh > 0 else 1]
+        return BB1.at[:, 4 if dh > 0 else 5], b1_vert.at[0 if dh > 0 else 1]
 
     b1_moves = near_copies(b1_send, b1_recv, b1_refs, UPDOWN)
     start(b1_moves)
-    start_far(q2_moves, False)
+
+    wait_recv(deep_moves)
+    build((*range(-7, -3), *range(11, 15)))
+    between((*range(-7, -3), *range(10, 14)))
+    for z in (*range(-6, -2), *range(10, 14)):
+        first_sweep(z)
+    second_sweep((*range(-5, -1), *range(9, 13)))
+    restrict((-2, -1, 4, 5))
 
     lane1 = iota((24, 128), 1)
     col1 = lane1 % 64
@@ -398,15 +410,12 @@
             if 0 <= z < 4:
                 DD1[t, z] = d
 
-    wait_recv(b1_moves)
-    start_far(q2_moves, True)
-    for t in range(2):
-        for z in range(3):
-            BB1[t, z] = jnp.where(below, b1_vert[0, t, z], 0.0)
-            BB1[t, z + 7] = jnp.where(above, b1_vert[1, t, z], 0.0)
-
-    for z in range(-3, 7):
+    for z in range(-2, 6):
         for t in range(2):
+            if z < 0:
+                BB1[t, z + 3] = jnp.where(below, BB1[t, z + 3], 0.0)
+            if z > 3:
+                BB1[t, z + 3] = jnp.where(above, BB1[t, z + 3], 0.0)
             VA1[t, z + 3] = WH1[t, z + 3] * BB1[t, z + 3]
 
     def apply1(v, off, t, z):
@@ -416,10 +425,15 @@
         e = HC1[0, z + 3] * pltpu.roll(x, 1, 1) + HC1[1, z + 3] * pltpu.roll(x, 127, 1)
         return x, (a + b + e) + (jnp.where(lane1 < 64, a, b) if t == 0 else e)
 
-    for z in range(-2, 6):
-        for t in range(2):
-            x, n = apply1(VA1, 3, t, z)
-            VB1[t, z + 2] = KEEP * x + WH1[t, z + 3] * (BB1[t, z + 3] + n)
+    def second_sweep1(zs):
+        for z in zs:
+            for t in range(2):
+                x, n = apply1(VA1, 3, t, z)
+                VB1[t, z + 2] = KEEP * x + WH1[t, z + 3] * (BB1[t, z + 3] + n)
+
+    second_sweep1(range(-1, 5))
+    down_a = one_hot((128, 128), lambda l, j: l // 2 == j)
+    down_b = one_hot((128, 128), lambda l, j: jnp.logical_and(l < 64, l // 2 == j - 64))
     for z in range(2):
         for t in range(2):
             total = None
@@ -428,12 +442,16 @@
                 r = BB1[t, 2 * z + k + 3] + n - DD1[t, 2 * z + k] * x
                 total = r[0:16] if total is None else total + r[0:16]
             RS1[t, z] = total
-    down_a = one_hot((128, 128), lambda l, j: l // 2 == j)
-    down_b = one_hot((128, 128), lambda l, j: jnp.logical_and(l < 64, l // 2 == j - 64))
-    b2_own[...] = (dot(row_pairs(RS1, 0, 8), down_a) + dot(row_pairs(RS1, 1, 8), down_b)).reshape(2, 8, 128)
+        b2_own[z] = dot(pairs(RS1, 0, z, 8), down_a) + dot(pairs(RS1, 1, z, 8), down_b)
     b2_moves = far_copies(b2_send, b2_recv, b2_own, b2)
     start(b2_moves)
     b2[pl.ds(2 * h, 2), 16:24] = b2_own[...]
+
+    wait_recv(b1_moves)
+    for t in range(2):
+        VA1[t, 0] = WH1[t, 0] * jnp.where(below, b1_vert[0, t], 0.0)
+        VA1[t, 9] = WH1[t, 9] * jnp.where(above, b1_vert[1, t], 0.0)
+    second_sweep1((-2, 5))
 
     lane2 = iota((40, 128), 1)
     row2 = iota((40, 128), 0)
@@ -530,18 +548,16 @@
 
     up_a = one_hot((128, 128), lambda l, j: l == j // 2)
     up_b = one_hot((128, 128), lambda l, j: jnp.logical_and(j < 64, l == 64 + j // 2))
-    coarse = PO2[pl.ds(2 * h, 4)].reshape(96, 128)
-    for t, m in enumerate((up_a, up_b)):
-        e = dot(coarse, m).reshape(4, 24, 128)
-        for k in range(4):
-            T1[t, k, pl.ds(0, 24, 2)] = e[k]
-            T1[t, k, pl.ds(1, 24, 2)] = e[k]
-    for z in range(-2, 6):
-        for t in range(2):
-            k = (z + 2) // 2
+    for k in range(4):
+        coarse = PO2[2 * h + k]
+        for t, m in enumerate((up_a, up_b)):
+            e = dot(coarse, m)
+            T1[t, k, pl.ds(0, 24, 2)] = e
+            T1[t, k, pl.ds(1, 24, 2)] = e
             tail = jnp.where(sub8 < 4, T1[t, k, 32:40], T1[t, k, 8:16])
             e = jnp.concatenate([T1[t, k, 16:32], tail], axis=0)
-            VB1[t, z + 2] = VB1[t, z + 2] + e
+            for z in (2 * k, 2 * k + 1):
+                VB1[t, z] = VB1[t, z] + e
     for z in range(-1, 5):
         for t in range(2):
             x, n = apply1(VB1, 2, t, z)
@@ -549,21 +565,20 @@
 
     up_lo = one_hot((128, 128), lambda l, j: l == j // 2)
     up_hi = one_hot((128, 128), lambda l, j: l == 64 + j // 2)
-    for c in range(3):
-        e = dot(PO1[c // 2].reshape(144, 128), up_hi if c == 1 else up_lo).reshape(6, 24, 128)
-        for k in range(6):
-            T0[c, k, pl.ds(0, 24, 2)] = e[k]
-            T0[c, k, pl.ds(1, 24, 2)] = e[k]
-    for z in range(-1, 9):
+    for k in range(6):
         for c in range(3):
-            k = (z + 2) // 2
-            V1[c, z + 1] = V1[c, z + 1] + T0[c, k]
+            e = dot(PO1[c // 2, k], up_hi if c == 1 else up_lo)
+            T0[c, k, pl.ds(0, 24, 2)] = e
+            T0[c, k, pl.ds(1, 24, 2)] = e
+            for z in (2 * k - 2, 2 * k - 1):
+                if -1 <= z < 9:
+                    V1[c, z + 5] = V1[c, z + 5] + T0[c, k]
     for z in range(8):
         for c in range(3):
-            x, n = apply0(V1, 1, c, z)
-            out[c, z] = (KEEP * x + WH[c, z + 2] * (BB[c, z + 2] + n))[0:32]
-
-    for moves in (label_moves, q1_moves, q2_moves, b1_moves, b2_moves):
+            x, n = apply0(V1, 5, c, z)
+            out[c, z] = (KEEP * x + WH[c, z + 6] * (BB[c, z + 6] + n))[0:32]
+
+    for moves in (label_moves, deep_moves, q1_moves, q2_moves, b1_moves, b2_moves):
         wait_send(moves)
 
 
@@ -577,15 +592,15 @@
     scratch = [
         pltpu.SMEM((3,), F32), pltpu.SMEM((3, 3), F32),
         vmem(8, 32, 128, dtype=i32), vmem(2, 32, 128, dtype=i32),
-        vmem(3, 32, 128, dtype=i32), vmem(3, 32, 128, dtype=i32),
-        vmem(2, 11, 8, 128, dtype=i32), vmem(2, 2, 3, 8, 128, dtype=i32), vmem(2, 11, 8, 128, dtype=i32),
+        vmem(7, 32, 128, dtype=i32), vmem(7, 32, 128, dtype=i32),
+        vmem(2, 11, 8, 128, dtype=i32), vmem(2, 2, 7, 8, 128, dtype=i32), vmem(2, 11, 8, 128, dtype=i32),
         vmem(4, 16, 128), vmem(2, 4, 16, 128), vmem(2, 3, 4, 4, 128), vmem(2, 4, 4, 128),
         vmem(8, 40, 128), vmem(2, 8, 128),
-        vmem(2, 2, 3, 24, 128),
+        vmem(2, 2, 24, 128),
         vmem(8, 40, 128), vmem(2, 8, 128),
-        vmem(14, 48, 128), vmem(3, 14, 48, 128), vmem(13, 48, 128), vmem(2, 12, 48, 128), vmem(2, 12, 48, 128),
-        vmem(3, 12, 48, 128), vmem(3, 12, 48, 128), vmem(3, 8, 48, 128), vmem(3, 12, 48, 128),
-        vmem(3, 10, 48, 128), vmem(3, 4, 48, 128), vmem(2, 2, 8, 128),
+        vmem(22, 48, 128), vmem(3, 22, 48, 128), vmem(21, 48, 128), vmem(2, 20, 48, 128), vmem(2, 20, 48, 128),
+        vmem(3, 20, 48, 128), vmem(3, 20, 48, 128), vmem(3, 16, 48, 128), vmem(3, 20, 48, 128),
+        vmem(3, 18, 48, 128), vmem(3, 8, 48, 128), vmem(2, 2, 8, 128),
         vmem(12, 24, 128), vmem(11, 24, 128), vmem(2, 10, 24, 128), vmem(2, 10, 24, 128), vmem(2, 10, 24, 128),
         vmem(2, 10, 24, 128), vmem(2, 4, 24, 128), vmem(2, 10, 24, 128), vmem(2, 8, 24, 128),
         vmem(2, 2, 16, 128), vmem(2, 6, 24, 128),
@@ -596,7 +611,7 @@
         vmem(3, 6, 48, 128), vmem(2, 4, 32, 128),
         pltpu.SemaphoreType.DMA((4,)),
     ]
-    for count in (8, 8, 19, 2, 19):
+    for count in (8, 6, 8, 19, 2, 19):
         scratch += [pltpu.SemaphoreType.DMA((count,)), pltpu.SemaphoreType.DMA((count,))]
 
     def local(material, clamped, stiffness_table, eigenstrain):

time: 25.6 us -> 23.3 us (0.910)
  Pallas kernels: 24.8 us -> 22.5 us
    pallas_call x1, Pallas kernels: 24.8 us -> 22.5 us  [local(): pl.pallas_call(functools.partial(kernel, heights, tiles), out_shape=jax.S...]
where the time goes in v5:
time: 23.3 us; the launch traced here: 23.2 us
  Pallas kernels  22.5 us (97%)
  local copies, waits for them, and re-layouts  0.75 us (3%)
    pallas_call x1, Pallas kernels, local(): pl.pallas_call(functools.partial(kernel, heights, tiles), out_shape=jax.S...  22.5 us
    unnamed x1, local copies, waits for them, and re-layouts  0.75 us

profile of v5, /device:TPU:103, one launch (start us, length us, event | category | flops | bytes accessed | tf_op | source)
XLA Modules:
  0.0 23.2 jit_solution(13617669084332292238)
XLA Ops:
  0.0 22.5 %shard_map.46 = f32[3,8,32,128]{3,2,1,0:T(8,128)S(1)} custom-call(s32[8,32,128]{2,1,0:T(8,128)} %mat_hbm.1, s32[8,32,128]{2,1,0:T(8,128)} %clamp_hbm.1, f32[3]{0:T(128)} %table_hbm.1, f32[3,3]{1,0:T(4,128)} %eigen_hbm.1), custom_call_target="tpu_custom_call" | custom-call | tf_op jit(solution)/shard_map/pallas_call | solution.py:618
  22.5 0.7 %copy.6 = f32[3,8,32,128]{3,2,1,0:T(8,128)} copy(f32[3,8,32,128]{3,2,1,0:T(8,128)S(1)} %shard_map.46) | data formatting | bytes 786432

commit v6 on v5

--- a/solution.py
+++ b/solution.py
@@ -63,6 +63,7 @@
     S3, HZ3, HR3, HC3, WH3, BB3, V3,
     T0, R4,
     local_sem,
+    met,
     m_send, m_recv, d_send, d_recv, q1_send, q1_recv, q2_send, q2_recv, b1_send, b1_recv, b2_send, b2_recv,
 ):
     i = lax.axis_index("tile")
@@ -84,14 +85,14 @@
 
     in_mat.start()
     barrier = pltpu.get_barrier_semaphore()
-    ring = [(dt, k) for dt in (-1, 1, 0) for k in (1, 3, 0) if (dt, k) != (0, 0)]
-    for dt, k in ring:
-        @pl.when(tile_ok(dt))
+    for dt, dh in NEAR:
+        @pl.when(near_ok(dt, dh))
         def _():
             pl.semaphore_signal(
-                barrier, inc=1, device_id=far_id(dt, k), device_id_type=pl.DeviceIdType.MESH
+                barrier, inc=1, device_id={"tile": i + dt, "height": h + dh},
+                device_id_type=pl.DeviceIdType.MESH,
             )
-    reach = 3 * (tile_ok(-1).astype(jnp.int32) + tile_ok(1).astype(jnp.int32)) + 2
+    reach = sum(near_ok(dt, dh).astype(jnp.int32) for dt, dh in NEAR)
 
     in_cl.start()
     in_table.start()
@@ -130,6 +131,21 @@
             )
             copies.append((copy, tile_ok(dt), tile_ok(-dt)))
         return copies
+
+    def start_far(copies, apart):
+        for (_, dh), (copy, sends, _) in zip(FAR, copies):
+            if dh == 1:
+                wide = h == heights - 1
+            elif dh == 3:
+                wide = h == 0
+            elif apart:
+                continue
+            else:
+                wide = h < 0
+
+            @pl.when(jnp.logical_and(sends, wide if apart else jnp.logical_not(wide)))
+            def _():
+                copy.start()
 
     def start(copies):
         for copy, sends, _ in copies:
@@ -233,7 +249,14 @@
     row = iota((48, 128), 0)
     sub8 = iota((8, 128), 0)
     wait_recv(label_moves)
-    start(q2_moves)
+    for dh in (-1, 1):
+        @pl.when(near_ok(0, dh))
+        def _():
+            pl.semaphore_signal(
+                met, inc=1, device_id={"tile": i, "height": h + dh},
+                device_id_type=pl.DeviceIdType.MESH,
+            )
+    start_far(q2_moves, False)
     below, above = h > 0, h < heights - 1
     before, after = i > 0, i < tiles - 1
 
@@ -363,6 +386,9 @@
     second_sweep((*range(-5, -1), *range(9, 13)))
     restrict((-2, -1, 4, 5))
 
+    pl.semaphore_wait(met, near_ok(0, -1).astype(jnp.int32) + near_ok(0, 1).astype(jnp.int32))
+    start_far(q2_moves, True)
+
     lane1 = iota((24, 128), 1)
     col1 = lane1 % 64
     wait_recv(q1_moves)
@@ -610,6 +636,7 @@
         vmem(4, 40, 128), vmem(2, 4, 40, 128),
         vmem(3, 6, 48, 128), vmem(2, 4, 32, 128),
         pltpu.SemaphoreType.DMA((4,)),
+        pltpu.SemaphoreType.REGULAR,
     ]
     for count in (8, 6, 8, 19, 2, 19):
         scratch += [pltpu.SemaphoreType.DMA((count,)), pltpu.SemaphoreType.DMA((count,))]

time: 23.3 us -> 23.4 us (level)
  no operation moved by 1% of the time
where the time goes in v6:
time: 23.4 us; the launch traced here: 23.3 us
  Pallas kernels  22.5 us (96%)
  local copies, waits for them, and re-layouts  0.75 us (3%)
    pallas_call x1, Pallas kernels, local(): pl.pallas_call(functools.partial(kernel, heights, tiles), out_shape=jax.S...  22.5 us
    unnamed x1, local copies, waits for them, and re-layouts  0.75 us

profile of v6, /device:TPU:103, one launch (start us, length us, event | category | flops | bytes accessed | tf_op | source)
XLA Modules:
  0.0 23.3 jit_solution(10911739285140192259)
XLA Ops:
  0.0 22.5 %shard_map.46 = f32[3,8,32,128]{3,2,1,0:T(8,128)S(1)} custom-call(s32[8,32,128]{2,1,0:T(8,128)} %mat_hbm.1, s32[8,32,128]{2,1,0:T(8,128)} %clamp_hbm.1, f32[3]{0:T(128)} %table_hbm.1, f32[3,3]{1,0:T(4,128)} %eigen_hbm.1), custom_call_target="tpu_custom_call" | custom-call | tf_op jit(solution)/shard_map/pallas_call | solution.py:645
  22.5 0.7 %copy.6 = f32[3,8,32,128]{3,2,1,0:T(8,128)} copy(f32[3,8,32,128]{3,2,1,0:T(8,128)S(1)} %shard_map.46) | data formatting | bytes 786432

commit v7 on v5

--- a/solution.py
+++ b/solution.py
@@ -537,9 +537,13 @@
         now, later = turn % 2, (turn + 1) % 2
         for z in range(4):
             x, n = apply2(V3.at[now], z, 4, 2, HZ3, HR3, HC3)
-            V3[later, z] = KEEP * x + WH3[z] * (BB3[z] + n)
+            new = KEEP * x + WH3[z] * (BB3[z] + n)
+            if turn == 0:
+                V3[later, z] = new
+            else:
+                V3[later, z, 8:32] = new[8:32]
     for z in range(8):
-        VB2[z] = VB2[z] + V3[1, z // 2]
+        VB2[z, 8:32] = VB2[z, 8:32] + V3[1, z // 2, 8:32]
     PO2[0] = jnp.zeros((24, 128), F32)
     PO2[9] = jnp.zeros((24, 128), F32)
     for z in range(8):

time: 23.3 us -> 23.3 us (level)
  no operation moved by 1% of the time
where the time goes in v7:
time: 23.3 us; the launch traced here: 23.2 us
  Pallas kernels  22.5 us (97%)
  local copies, waits for them, and re-layouts  0.75 us (3%)
    pallas_call x1, Pallas kernels, local(): pl.pallas_call(functools.partial(kernel, heights, tiles), out_shape=jax.S...  22.5 us
    unnamed x1, local copies, waits for them, and re-layouts  0.75 us

profile of v7, /device:TPU:103, one launch (start us, length us, event | category | flops | bytes accessed | tf_op | source)
XLA Modules:
  0.0 23.2 jit_solution(7366362383312451440)
XLA Ops:
  0.0 22.5 %shard_map.46 = f32[3,8,32,128]{3,2,1,0:T(8,128)S(1)} custom-call(s32[8,32,128]{2,1,0:T(8,128)} %mat_hbm.1, s32[8,32,128]{2,1,0:T(8,128)} %clamp_hbm.1, f32[3]{0:T(128)} %table_hbm.1, f32[3,3]{1,0:T(4,128)} %eigen_hbm.1), custom_call_target="tpu_custom_call" | custom-call | tf_op jit(solution)/shard_map/pallas_call | solution.py:622
  22.5 0.7 %copy.6 = f32[3,8,32,128]{3,2,1,0:T(8,128)} copy(f32[3,8,32,128]{3,2,1,0:T(8,128)S(1)} %shard_map.46) | data formatting | bytes 786432

commit v8 on v7

--- a/solution.py
+++ b/solution.py
@@ -306,13 +306,15 @@
         g2 = jnp.where(lane > 0, pltpu.roll(x, 1, 1), 0.0) - jnp.where(
             lane < 127, pltpu.roll(x, 127, 1), 0.0
         )
-        for c, g in enumerate((g0, g1, g2)):
-            d = total + f[c]
-            w = jnp.where(s > 0.0, OMEGA / jnp.where(s > 0.0, d, 1.0), 0.0)
+        d = [total + f[c] for c in range(3)]
+        d01 = d[0] * d[1]
+        one = jnp.where(s > 0.0, OMEGA / (d01 * d[2]), 0.0)
+        part = one * d[2]
+        for c, (g, w) in enumerate(((g0, part * d[1]), (g1, part * d[0]), (g2, one * d01))):
             BB[c, z + 6] = g
             WH[c, z + 6] = w
             if -4 <= z < 12:
-                DD[c, z + 4] = d
+                DD[c, z + 4] = d[c]
             V0[c, z + 6] = w * g
 
     for z in range(-2, 10):

time: 23.3 us -> 23.4 us (level)
  no operation moved by 1% of the time
where the time goes in v8:
time: 23.4 us; the launch traced here: 23.3 us
  Pallas kernels  22.5 us (96%)
  local copies, waits for them, and re-layouts  0.75 us (3%)
    pallas_call x1, Pallas kernels, local(): pl.pallas_call(functools.partial(kernel, heights, tiles), out_shape=jax.S...  22.5 us
    unnamed x1, local copies, waits for them, and re-layouts  0.75 us

profile of v8, /device:TPU:103, one launch (start us, length us, event | category | flops | bytes accessed | tf_op | source)
XLA Modules:
  0.0 23.3 jit_solution(9039042591281426903)
XLA Ops:
  0.0 22.5 %shard_map.46 = f32[3,8,32,128]{3,2,1,0:T(8,128)S(1)} custom-call(s32[8,32,128]{2,1,0:T(8,128)} %mat_hbm.1, s32[8,32,128]{2,1,0:T(8,128)} %clamp_hbm.1, f32[3]{0:T(128)} %table_hbm.1, f32[3,3]{1,0:T(4,128)} %eigen_hbm.1), custom_call_target="tpu_custom_call" | custom-call | tf_op jit(solution)/shard_map/pallas_call | solution.py:624
  22.5 0.7 %copy.6 = f32[3,8,32,128]{3,2,1,0:T(8,128)} copy(f32[3,8,32,128]{3,2,1,0:T(8,128)S(1)} %shard_map.46) | data formatting | bytes 786432
